TPU v7x, 512 devices: a whole 4x4x16 slice. The times are simulated.
512 devices in a mesh: req: 32 (over z, core), tensor: 16 (over y, x).
Axes of the slice: x: 4, y: 4, z: 16, core: 2. Of those that a mesh axis runs over, the one named last changes fastest.
Arguments:
- text: bfloat16 [12288, 4096], P('req', 'tensor'), may hold values from -6 to 6
- patches: bfloat16 [1024, 6, 6, 4096], P('req', None, None, 'tensor'), may hold values from -6 to 6
- grids: int32 [1024, 2], replicated, may hold values from 2 to 6, as said below
- image_request: int32 [1024], replicated, may hold values from 0 to 31, as said below
- slot_start: int32 [1024], replicated, may hold values from 1 to 375, as said below
- vis_gain: bfloat16 [4096], P('tensor'), may hold values from 0.099609375 to 1.8984375
- dec_gain: bfloat16 [4096], replicated, may hold values from 0.099609375 to 1.8984375
- w_qkv: bfloat16 [4096, 3, 2048], P(None, None, 'tensor'), may hold values from -0.09375 to 0.09375
- w_out: bfloat16 [2048, 4096], P('tensor'), may hold values from -0.125 to 0.125
Outputs:
- layer_out: bfloat16 [12288, 4096], P('req', 'tensor')
Inputs may be any that keep to these rules, and one draw needn't show every extreme that they name: `grids`: heights and widths are even; some image has a 6 x 6 grid and some a 2 x 2 grid. `image_request`: the images of one index of req go to distinct requests, one to each. `slot_start`: the regions of 9 positions of the images of one request don't intersect and lie within the prompt; position 0 of every prompt lies outside them.
All inputs are finite; a program needn't handle non-finite values.
Results may differ from a plain program's by a relative error of at most 0.011.
Values may be sent and summed in bfloat16 or wider, within the bound.
A program may use at most 64 MiB of HBM per device.

v0:
```python
import jax
import jax.numpy as jnp
from jax import lax
from jax.sharding import PartitionSpec as P

D = 4096
HD = 128


def pool_blocks(block):
    lead = block.shape[:-3]
    side = block.shape[-3]
    width = block.shape[-1]
    half = side // 2
    shaped = block.astype(jnp.float32).reshape(lead + (half, 2, half, 2, width))
    return shaped.mean(axis=(-4, -2)).reshape(lead + (half * half, width))


def body(text, patches, grids, image_request, slot_start, vis_gain, dec_gain, w_qkv, w_out):
    n_req = lax.axis_size("req")
    me_req = lax.axis_index("req")
    me_ten = lax.axis_index("tensor")
    img_dev, side, _, width = patches.shape
    half = side // 2
    region = half * half
    length = text.shape[0]
    gain_v = vis_gain.astype(jnp.float32)
    req_map = image_request.reshape(n_req, img_dev)
    pick = req_map == me_req
    has_img = jnp.any(pick, axis=1)
    start_src = jnp.sum(jnp.where(pick, slot_start.reshape(n_req, img_dev), 0), axis=1)
    grid_src = jnp.sum(jnp.where(pick[:, :, None], grids.reshape(n_req, img_dev, 2), 0), axis=1)
    own_map = lax.dynamic_slice_in_dim(image_request, me_req * img_dev, img_dev)
    onehot = (jnp.arange(n_req, dtype=jnp.int32)[:, None] == own_map[None, :]).astype(jnp.bfloat16)
    outgoing = jnp.einsum(
        "nk,kabw->nabw", onehot, patches, preferred_element_type=jnp.float32
    ).astype(jnp.bfloat16)
    received = lax.all_to_all(outgoing, "req", split_axis=0, concat_axis=0, tiled=True)
    pooled = pool_blocks(received)
    sums = lax.psum(jnp.sum(pooled * pooled, axis=-1), "tensor")
    arrived = (pooled * lax.rsqrt(sums / D + 1e-05)[..., None] * gain_v).astype(jnp.bfloat16)
    cells = jnp.arange(region, dtype=jnp.int32)
    row_i = cells // half
    col_j = cells % half
    height = grid_src[:, 0][:, None] // 2
    grid_w = grid_src[:, 1][:, None] // 2
    valid = has_img[:, None] & (row_i[None, :] < height) & (col_j[None, :] < grid_w)
    pos = jnp.where(valid, start_src[:, None] + row_i[None, :] * grid_w + col_j[None, :], length)
    rpos = jnp.where(has_img[:, None], start_src[:, None] + cells[None, :], length)
    img_rows = (
        jnp.zeros((length, width), jnp.bfloat16)
        .at[pos.reshape(-1)]
        .set(arrived.reshape(-1, width), mode="drop")
    )
    is_img = jnp.zeros((length,), bool).at[pos.reshape(-1)].set(True, mode="drop")
    in_region = jnp.zeros((length,), bool).at[rpos.reshape(-1)].set(True, mode="drop")
    key_ok = ~in_region | is_img
    x_in = jnp.where(is_img[:, None], img_rows, text)
    xf = x_in.astype(jnp.float32)
    heads_cols = w_qkv.shape[2]
    w_flat = w_qkv.reshape(w_qkv.shape[0], 3 * heads_cols)
    gain_d = dec_gain.astype(jnp.float32)
    sums_rows = lax.psum(jnp.sum(xf * xf, axis=-1), "tensor")
    gain_part = lax.dynamic_slice_in_dim(gain_d, me_ten * width, width)
    normed = (xf * lax.rsqrt(sums_rows / D + 1e-05)[:, None] * gain_part).astype(jnp.bfloat16)
    qkv = jnp.dot(
        lax.all_gather(normed, "tensor", axis=1, tiled=True),
        w_flat,
        preferred_element_type=jnp.float32,
    )
    heads_here = heads_cols // HD
    qkv = qkv.astype(jnp.bfloat16).reshape(length, 3, heads_here, HD)
    scores = jnp.einsum("qhd,khd->hqk", qkv[:, 0], qkv[:, 1], preferred_element_type=jnp.float32)
    scores = scores / jnp.sqrt(jnp.float32(HD))
    causal = jnp.arange(length)[:, None] >= jnp.arange(length)[None, :]
    mask = causal & key_ok[None, :]
    scores = jnp.where(mask[None], scores, jnp.float32(-1e30))
    top = jnp.max(scores, axis=-1, keepdims=True)
    expo = jnp.exp(scores - top)
    probs = (expo / jnp.sum(expo, axis=-1, keepdims=True)).astype(jnp.bfloat16)
    context = jnp.einsum("hqk,khd->qhd", probs, qkv[:, 2], preferred_element_type=jnp.float32)
    context = context.astype(jnp.bfloat16).reshape(length, heads_cols)
    partial_value = jnp.dot(context, w_out, preferred_element_type=jnp.float32)
    summed = lax.psum_scatter(
        partial_value.astype(jnp.bfloat16), "tensor", scatter_dimension=1, tiled=True
    ).astype(jnp.float32)
    return (xf + summed).astype(jnp.bfloat16)


def solution(mesh):
    in_specs = (
        P("req", "tensor"),
        P("req", None, None, "tensor"),
        P(),
        P(),
        P(),
        P("tensor"),
        P(),
        P(None, None, "tensor"),
        P("tensor", None),
    )
    out_specs = P("req", "tensor")
    return jax.shard_map(body, mesh=mesh, in_specs=in_specs, out_specs=out_specs, check_vma=False)
```

profile of v0, /device:TPU:1, one launch (start us, length us, event | category | flops | bytes accessed | tf_op | source)
XLA Modules:
  0.0 313.4 jit_solution(3804294805305117140)
XLA Ops:
  6.6 0.9 dynamic_slice.6
  7.4 1.4 convolution_convert_fusion.1
  8.8 1.2 copy.19
  10.0 16.9 %all-to-all-start = ((bf16[32,6,6,256]{3,2,1,0:T(8,128)(2,1)}), bf16[32,6,6,256]{3,2,1,0:T(8,128)(2,1)S(1)}, u32[]{:S(2)}, u32[]{:S(2)}) async-start(bf16[32,6,6,256]{3,2,1,0:T(8,128)(2,1)} %copy.19), calls=%async_computation | async-start | bytes 1572864 | tf_op jit(solution)/shard_map/all_to_all | solution.py:38
  28.8 1.6 scatter_custom_fusion
  30.4 0.8 dynamic-slice_convert_fusion
  31.2 40.4 %all-to-all-done = bf16[32,6,6,256]{3,2,1,0:T(8,128)(2,1)S(1)} async-done(((bf16[32,6,6,256]{3,2,1,0:T(8,128)(2,1)}), bf16[32,6,6,256]{3,2,1,0:T(8,128)(2,1)S(1)}, u32[]{:S(2)}, u32[]{:S(2)}) %all-to-all-start) | async-done | bytes 589856 | tf_op jit(solution)/shard_map/all_to_all | solution.py:38
  71.5 0.2 copy.20
  71.9 0.2 copy.21
  72.2 34.3 %psum.14 = f32[32,9]{0,1:T(8,128)S(1)} all-reduce(f32[32,9]{0,1:T(8,128)S(1)} %reduce_sum.63), channel_id=1, replica_groups=mesh['req'=32,'tensor'=16] {'tensor'}, use_global_device_ids=true, to_apply=%region_6.7 | all-reduce | flops 288 | bytes 2304 | tf_op jit(solution)/shard_map/psum | solution.py:40
  106.7 0.1 reduce_sum.61
  106.9 1.7 scatter_custom_fusion.1
  108.6 0.3 fusion.4
  108.8 28.5 %psum.15 = f32[384]{0:T(512)S(1)} all-reduce(f32[384]{0:T(512)S(1)} %get-tuple-element.7), channel_id=1, replica_groups=mesh['req'=32,'tensor'=16] {'tensor'}, use_global_device_ids=true, to_apply=%region_9.10 | all-reduce | flops 384 | bytes 3072 | tf_op jit(solution)/shard_map/psum | solution.py:63
  137.4 0.8 fusion.6
  138.2 1.6 scatter_custom_fusion.2
  139.9 4.8 %copy.25 = bf16[4096,3,128]{0,2,1:T(8,128)(2,1)} copy(bf16[4096,3,128]{2,0,1:T(8,128)(2,1)} %param.16) | data formatting | bytes 6291456 | tf_op args[7]
  144.6 62.4 %all-gather.2.cloned.1.call-done = bf16[384,4096]{1,0:T(8,128)(2,1)} async-done(((bf16[384,256]{1,0:T(8,128)(2,1)}), bf16[384,4096]{1,0:T(8,128)(2,1)}) %all-gather.2.cloned.1.call-update) | async-done | bytes 3145744 | tf_op jit(solution)/shard_map/all_gather | solution.py:67
  207.0 4.6 %convolution_convert_fusion.2 = bf16[384,384]{0,1:T(8,128)(2,1)S(1)} fusion(bf16[384,4096]{1,0:T(8,128)(2,1)} %all-gather.2.cloned.1.call-done, bf16[4096,384]{0,1:T(8,128)(2,1)} %bitcast.46), kind=kOutput, calls=%fused_computation.7 | convolution fusion | flops 1208107008 | bytes 6586368 | tf_op jit(solution)/shard_map/dot_general | solution.py:66
  211.7 0.3 fusion.27
  212.0 0.1 fusion.3
  212.1 2.9 convolution_convert_fusion
  215.0 89.9 %reduce-scatter.2.cloned.1.call-done = bf16[384,256]{1,0:T(8,128)(2,1)} async-done(((bf16[384,4096]{1,0:T(8,128)(2,1)}), bf16[384,256]{1,0:T(8,128)(2,1)}) %reduce-scatter.2.cloned.1.call-update) | async-done | bytes 196624 | tf_op jit(solution)/shard_map/reduce_scatter | solution.py:84
  304.9 1.6 fusion.7
  (51 shorter events, 2.3 us)
Async XLA Ops:
  6.5 205.6 %copy-start = (bf16[128,4096]{1,0:T(8,128)(2,1)S(1)}, bf16[128,4096]{1,0:T(8,128)(2,1)}, u32[]{:S(2)}) copy-start(bf16[128,4096]{1,0:T(8,128)(2,1)} %param.17) | copy-start | bytes 3145732
  6.5 20.4 %copy-start.4 = (s32[1024]{0:T(1024)S(1)}, s32[1024]{0:T(1024)}, u32[]{:S(2)}) copy-start(s32[1024]{0:T(1024)} %param.12) | copy-start | bytes 12292
  6.5 20.4 %copy-start.5 = (bf16[256]{0:T(256)(128)(2,1)S(1)}, bf16[256]{0:T(256)(128)(2,1)}, u32[]{:S(2)}) copy-start(bf16[256]{0:T(256)(128)(2,1)} %param.14) | copy-start | bytes 1540
  6.5 21.1 %copy-start.3 = (s32[1024]{0:T(1024)S(1)}, s32[1024]{0:T(1024)}, u32[]{:S(2)}) copy-start(s32[1024]{0:T(1024)} %param.13) | copy-start | bytes 12292
  6.5 21.6 %copy-start.2 = (s32[1024,2]{0,1:T(2,128)S(1)}, s32[1024,2]{0,1:T(2,128)}, u32[]{:S(2)}) copy-start(s32[1024,2]{0,1:T(2,128)} %param.11) | copy-start | bytes 24580
  10.0 98.6 %copy-start.1 = (bf16[384,256]{1,0:T(8,128)(2,1)S(1)}, bf16[384,256]{1,0:T(8,128)(2,1)}, u32[]{:S(2)}) copy-start(bf16[384,256]{1,0:T(8,128)(2,1)} %param.9) | copy-start | bytes 589828
  10.0 61.5 %all-to-all-start = ((bf16[32,6,6,256]{3,2,1,0:T(8,128)(2,1)}), bf16[32,6,6,256]{3,2,1,0:T(8,128)(2,1)S(1)}, u32[]{:S(2)}, u32[]{:S(2)}) async-start(bf16[32,6,6,256]{3,2,1,0:T(8,128)(2,1)} %copy.19), calls=%async_computation | async-start | bytes 1572864 | tf_op jit(solution)/shard_map/all_to_all | solution.py:38
  26.9 180.1 %all-gather.2.cloned.1.call-start = ((), (), s32[]{:S(2)}) async-start(), calls=%async_computation.2 | async-start | bytes 3342336 | tf_op jit(solution)/shard_map/all_gather | solution.py:67
  138.2 166.7 %reduce-scatter.2.cloned.1.call-start = ((), (), s32[]{:S(2)}) async-start(), calls=%async_computation.3 | async-start | bytes 3342336 | tf_op jit(solution)/shard_map/reduce_scatter | solution.py:84
Sparse Core Ops, SparseCore 0:
  138.3 68.6 all-gather.1
  215.1 89.6 reduce-scatter.1
where the time goes:
time: 314 us; the launch traced here: 313 us
  waiting for transfers between devices  193 us (61%)
  blocking collectives  62.8 us (20%)
  starting transfers between devices  17 us (5%)
  between operations  13.7 us (4%)
  local copies, waits for them, and re-layouts  12.1 us (4%)
  matrix products  9.21 us (3%)
  other arithmetic  5.97 us (2%)
    reduce_scatter x1, waiting for transfers between devices, body(): lax.psum_scatter(partial_value.astype(jnp.bfloat16), 'tensor', scatter_di...  89.9 us
    all_gather x1, waiting for transfers between devices, body(): lax.all_gather(normed, 'tensor', axis=1, tiled=True)  62.4 us
    all_to_all x1, waiting for transfers between devices, body(): lax.all_to_all(outgoing, 'req', split_axis=0, concat_axis=0, tiled=True)  40.4 us
    psum x1, blocking collectives, body(): sums = lax.psum(jnp.sum(pooled * pooled, axis=-1), 'tensor')  34.3 us
    psum x1, blocking collectives, body(): sums_rows = lax.psum(jnp.sum(xf * xf, axis=-1), 'tensor')  28.5 us
    all_to_all x1, starting transfers between devices, body(): lax.all_to_all(outgoing, 'req', split_axis=0, concat_axis=0, tiled=True)  16.9 us
  transfers between devices with their start and end apart: 3, of which 3 were waited for; matrix products, arithmetic and copies ran while one was open for 3% of the time, Pallas kernels for 0%

commit v1 on v0

v1 whole, which is shorter than its diff:
```python
import functools

import jax
import jax.numpy as jnp
from jax import lax
from jax.experimental import pallas as pl
from jax.experimental.pallas import tpu as pltpu
from jax.sharding import PartitionSpec as P

D = 4096
HD = 128
L = 384
W = 256
NR = 32
NT = 16
IMG = 32
CELLS = 9
SLOT = 24
ROWS = L + 8
EPS = 1e-05
MESH = pl.DeviceIdType.MESH
F32 = jnp.float32
BF16 = jnp.bfloat16


def iota(shape, dim):
    return lax.broadcasted_iota(jnp.int32, shape, dim)


def dot(a, b):
    return lax.dot_general(a, b, (((1,), (0,)), ((), ())), preferred_element_type=F32)


def dot_nt(a, b):
    return lax.dot_general(a, b, (((1,), (1,)), ((), ())), preferred_element_type=F32)


def kernel(
    text_h, patch_h, grid_r, req_r, slot_r, gv_r, gd_r, wqkv_h, wout_h, out_r,
    text_v, patch_v, w_v, wcol, stage_f, stage, recv, recv_f, place, rcat, xraw_v, xfull, cfull,
    acc, oacc, loc_sem, w_send, w_recv, a_send, a_recv, x_send, x_recv, c_send, c_recv,
):
    me_r = lax.axis_index("req")
    me_t = lax.axis_index("tensor")

    load_p = pltpu.make_async_copy(patch_h, patch_v, loc_sem.at[0])
    load_t = pltpu.make_async_copy(text_h, text_v, loc_sem.at[1])
    load_w = [
        pltpu.make_async_copy(wqkv_h.at[j], w_v.at[:, pl.ds(j * HD, HD)], loc_sem.at[2 + j])
        for j in range(3)
    ]
    own_cols = pl.ds(pl.multiple_of(me_t * W, W), W)
    load_o = pltpu.make_async_copy(wout_h.at[:, own_cols], wcol.at[me_t], loc_sem.at[5])
    load_p.start()
    barrier = pltpu.get_barrier_semaphore()

    def greet_r(d, _):
        pl.semaphore_signal(
            barrier, inc=1, device_id={"req": lax.rem(me_r + d, NR)}, device_id_type=MESH
        )
        return _

    def greet_t(d, _):
        pl.semaphore_signal(
            barrier, inc=1, device_id={"tensor": lax.rem(me_t + d, NT)}, device_id_type=MESH
        )
        return _

    lax.fori_loop(1, NR, greet_r, 0)
    lax.fori_loop(1, NT, greet_t, 0)
    load_t.start()
    for copy in load_w:
        copy.start()
    load_o.start()

    lane = iota((1, NR * IMG), 1)
    req = req_r[...]
    own_sel = (iota((IMG, NR * IMG), 1) == me_r * IMG + iota((IMG, NR * IMG), 0)).astype(BF16)
    req8 = jnp.broadcast_to(req.astype(F32), (8, NR * IMG)).astype(BF16)
    own = dot_nt(req8, own_sel)[0:1, :]
    onehot = (iota((NR, IMG), 0).astype(F32) == own).astype(BF16)
    load_p.wait()
    stage_f[...] = jnp.zeros_like(stage_f)
    for c in range(CELLS):
        i, j = 2 * (c // 3), 2 * (c % 3)
        total = (
            patch_v[i, j].astype(F32) + patch_v[i, j + 1].astype(F32)
            + patch_v[i + 1, j].astype(F32) + patch_v[i + 1, j + 1].astype(F32)
        )
        sent = dot(onehot, (total * 0.25).astype(BF16))
        stage_f[pl.ds(c, NR, stride=SLOT), :] = sent[:, :HD]
        stage_f[pl.ds(CELLS + c, NR, stride=SLOT), :] = sent[:, HD:]
    stage[...] = stage_f[...].astype(BF16).reshape(NR, SLOT, HD)

    pl.semaphore_wait(barrier, NR - 1 + NT - 1)

    def a_copy(d):
        to = lax.rem(me_r + d, NR)
        return pltpu.make_async_remote_copy(
            src_ref=stage.at[to], dst_ref=recv.at[me_r], send_sem=a_send.at[d],
            recv_sem=a_recv.at[me_r], device_id={"req": to}, device_id_type=MESH,
        )

    def a_wait(d):
        frm = lax.rem(me_r + d, NR)
        pltpu.make_async_remote_copy(
            src_ref=stage.at[frm], dst_ref=recv.at[frm], send_sem=a_send.at[d],
            recv_sem=a_recv.at[frm], device_id={"req": frm}, device_id_type=MESH,
        ).wait_recv()

    def w_copy(d):
        to = lax.rem(me_t + d, NT)
        cols = pl.ds(pl.multiple_of(to * W, W), W)
        return pltpu.make_async_remote_copy(
            src_ref=wout_h.at[:, cols], dst_ref=wcol.at[me_t], send_sem=w_send.at[d],
            recv_sem=w_recv.at[me_t], device_id={"tensor": to}, device_id_type=MESH,
        )

    def t_copy(buf, send, rec, d):
        to = lax.rem(me_t + d, NT)
        return pltpu.make_async_remote_copy(
            src_ref=buf.at[me_t], dst_ref=buf.at[me_t], send_sem=send.at[d],
            recv_sem=rec.at[me_t], device_id={"tensor": to}, device_id_type=MESH,
        )

    def t_wait(buf, send, rec, d):
        frm = lax.rem(me_t + d, NT)
        pltpu.make_async_remote_copy(
            src_ref=buf.at[frm], dst_ref=buf.at[frm], send_sem=send.at[d],
            recv_sem=rec.at[frm], device_id={"tensor": frm}, device_id_type=MESH,
        ).wait_recv()
        return frm

    def loop(lo, hi, f):
        def step(d, _):
            f(d)
            return _
        lax.fori_loop(lo, hi, step, 0)

    loop(1, NR, lambda d: a_copy(d).start())
    loop(1, NT, lambda d: w_copy(d).start())
    recv[me_r] = stage[me_r]

    row = iota((8, NR * IMG), 0)
    start = jnp.broadcast_to(slot_r[...], (8, NR * IMG))
    half_h = jnp.broadcast_to(grid_r[0:1, :], (8, NR * IMG)) // 2
    half_w = jnp.broadcast_to(grid_r[1:2, :], (8, NR * IMG)) // 2
    facts = jnp.where(
        row == 0, start // 16, jnp.where(row == 1, start % 16, jnp.where(row == 2, half_h, half_w))
    )
    facts = jnp.where(jnp.broadcast_to(req, (8, NR * IMG)) == me_r, facts, 0).astype(F32).astype(BF16)
    seg = (iota((NR, NR * IMG), 1) // IMG == iota((NR, NR * IMG), 0)).astype(BF16)
    by_lane = dot_nt(facts, seg)
    by_row = dot_nt(seg, facts)
    start_l = by_lane[0:1, :] * 16.0 + by_lane[1:2, :]
    hh_l, hw_l = by_lane[2:3, :], by_lane[3:4, :]
    position = iota((L, NR), 0).astype(F32)
    hits = jnp.zeros((L, NR), F32)
    for c in range(CELLS):
        i, j = float(c // 3), float(c % 3)
        pos = jnp.where((hh_l > i) & (hw_l > j), start_l + i * hw_l + j, -1.0)
        hit = (position == pos).astype(F32)
        hits = hits + hit
        place[:, c * NR:(c + 1) * NR] = hit.astype(BF16)
    is_img = jnp.sum(hits, axis=1, keepdims=True) > 0.5
    start_c = by_row[:, 0:1] * 16.0 + by_row[:, 1:2]
    filled_c = by_row[:, 2:3] * by_row[:, 3:4]
    off = iota((NR, L), 1).astype(F32) - start_c
    img_l = jnp.max(((off >= 0.0) & (off < filled_c)).astype(F32), axis=0, keepdims=True)
    bad_l = jnp.max(((off >= filled_c) & (off < float(CELLS))).astype(F32), axis=0, keepdims=True)

    load_t.wait()
    gv = gv_r[...].astype(F32)
    gd = gd_r[:, own_cols].astype(F32)

    loop(1, NR, a_wait)
    recv_f[...] = recv[...].reshape(NR * SLOT, HD).astype(F32)
    for c in range(CELLS):
        rcat[c * NR:(c + 1) * NR, :HD] = recv_f[pl.ds(c, NR, stride=SLOT), :].astype(BF16)
        rcat[c * NR:(c + 1) * NR, HD:] = recv_f[pl.ds(CELLS + c, NR, stride=SLOT), :].astype(BF16)
    img = dot(place[...], rcat[...])
    xraw = jnp.where(is_img, img * gv, text_v[...].astype(F32))
    xraw_v[...] = xraw
    xfull[me_t, :L, :] = (xraw * gd).astype(BF16)
    ones = jnp.ones((8, W), BF16)
    s_img = dot_nt(ones, (img * img).astype(BF16))
    s_row = dot_nt(ones, (xraw * xraw).astype(BF16))

    def two(s, r):
        hi = s.astype(BF16).astype(F32)
        lo = s - hi
        def wide(v):
            return jnp.concatenate([v[:, W:], jnp.zeros((8, 2 * W - L), F32)], axis=1)
        return jnp.where(
            r == 0, hi[:, :W], jnp.where(r == 1, wide(hi), jnp.where(r == 2, lo[:, :W], wide(lo)))
        )

    r8 = iota((8, W), 0)
    xfull[me_t, L:, :] = jnp.where(r8 < 4, two(s_img, r8), two(s_row, r8 - 4)).astype(BF16)

    loop(1, NT, lambda d: t_copy(xfull, x_send, x_recv, d).start())
    for copy in load_w:
        copy.wait()
    load_o.wait()

    def project(t):
        rows = pl.ds(pl.multiple_of(t * W, W), W)
        return dot(xfull[t, :L, :], w_v[rows, :])

    acc[...] = project(me_t)

    def gather_x(d, sums):
        t = t_wait(xfull, x_send, x_recv, d)
        acc[...] += project(t)
        return sums + xfull[t, L:, :].astype(F32)

    sums = lax.fori_loop(1, NT, gather_x, xfull[me_t, L:, :].astype(F32))

    def whole(r):
        return jnp.concatenate(
            [sums[r:r + 1, :] + sums[r + 2:r + 3, :],
             sums[r + 1:r + 2, :L - W] + sums[r + 3:r + 4, :L - W]], axis=1
        )

    s1, s2 = whole(0), whole(4)
    rv = jnp.where(img_l > 0.5, lax.rsqrt(s1 / D + EPS), 1.0)
    rd = lax.rsqrt(rv * rv * s2 / D + EPS)
    r8l = iota((8, L), 0)
    cols = jnp.transpose(jnp.where(r8l == 0, rv * rd, rv))
    scale_c, rv_c = cols[:, 0:1], cols[:, 1:2]
    qkv = (acc[...] * scale_c).astype(BF16)
    scores = dot_nt(qkv[:, :HD], qkv[:, HD:2 * HD]) * (HD ** -0.5)
    keep = (iota((L, L), 0) >= iota((L, L), 1)) & (bad_l < 0.5)
    scores = jnp.where(keep, scores, -1e30)
    top = jnp.max(scores, axis=-1, keepdims=True)
    expo = jnp.exp(scores - top)
    probs = (expo / jnp.sum(expo, axis=-1, keepdims=True)).astype(BF16)
    cfull[me_t] = dot(probs, qkv[:, 2 * HD:]).astype(BF16)
    loop(1, NT, lambda d: t_copy(cfull, c_send, c_recv, d).start())
    oacc[...] = dot(cfull[me_t], wcol[me_t])

    def gather_c(d):
        t_wait(wcol, w_send, w_recv, d)
        t = t_wait(cfull, c_send, c_recv, d)
        oacc[...] += dot(cfull[t], wcol[t])

    loop(1, NT, gather_c)
    x_in = (xraw_v[...] * rv_c).astype(BF16).astype(F32)
    out_r[...] = (x_in + oacc[...]).astype(BF16)

    loop(1, NR, lambda d: a_copy(d).wait_send())
    loop(1, NT, lambda d: w_copy(d).wait_send())
    loop(1, NT, lambda d: t_copy(xfull, x_send, x_recv, d).wait_send())
    loop(1, NT, lambda d: t_copy(cfull, c_send, c_recv, d).wait_send())


def body(text, patches, grids, image_request, slot_start, vis_gain, dec_gain, w_qkv, w_out):
    vmem = pl.BlockSpec(memory_space=pltpu.VMEM)
    hbm = pl.BlockSpec(memory_space=pl.ANY)
    dma = pltpu.SemaphoreType.DMA
    return pl.pallas_call(
        kernel,
        out_shape=jax.ShapeDtypeStruct((L, W), BF16),
        in_specs=[hbm, hbm, vmem, vmem, vmem, vmem, vmem, hbm, hbm],
        out_specs=vmem,
        scratch_shapes=[
            pltpu.VMEM((L, W), BF16),
            pltpu.VMEM((6, 6, IMG, W), BF16),
            pltpu.VMEM((D, 3 * HD), BF16),
            pltpu.VMEM((NT, HD, W), BF16),
            pltpu.VMEM((NR * SLOT, HD), F32),
            pltpu.VMEM((NR, SLOT, HD), BF16),
            pltpu.VMEM((NR, SLOT, HD), BF16),
            pltpu.VMEM((NR * SLOT, HD), F32),
            pltpu.VMEM((L, CELLS * NR), BF16),
            pltpu.VMEM((CELLS * NR, W), BF16),
            pltpu.VMEM((L, W), F32),
            pltpu.VMEM((NT, ROWS, W), BF16),
            pltpu.VMEM((NT, L, HD), BF16),
            pltpu.VMEM((L, 3 * HD), F32),
            pltpu.VMEM((L, W), F32),
            dma((6,)), dma((NT,)), dma((NT,)), dma((NR,)), dma((NR,)),
            dma((NT,)), dma((NT,)), dma((NT,)), dma((NT,)),
        ],
        compiler_params=pltpu.CompilerParams(
            collective_id=0, has_side_effects=True, vmem_limit_bytes=48 * 2**20
        ),
    )(
        text,
        patches.transpose(1, 2, 0, 3),
        grids.T,
        image_request.reshape(1, -1),
        slot_start.reshape(1, -1),
        vis_gain.reshape(1, -1),
        dec_gain.reshape(1, -1),
        w_qkv.transpose(1, 0, 2),
        w_out,
    )


def solution(mesh):
    in_specs = (
        P("req", "tensor"),
        P("req", None, None, "tensor"),
        P(),
        P(),
        P(),
        P("tensor"),
        P(),
        P(None, None, "tensor"),
        P("tensor", None),
    )
    return jax.shard_map(
        body, mesh=mesh, in_specs=in_specs, out_specs=P("req", "tensor"), check_vma=False
    )
```

time: 314 us -> 121 us (0.39)
  waiting for transfers between devices: 193 us -> 0 us
  Pallas kernels: 0 us -> 112 us
  blocking collectives: 62.8 us -> 0 us
  starting transfers between devices: 17 us -> 0 us
  between operations: 13.7 us -> 0.03 us
  matrix products: 9.21 us -> 0 us
  other arithmetic: 5.97 us -> 0 us
    pallas_call x0 -> x1, Pallas kernels: none -> 112 us  [body(): pl.pallas_call(kernel, out_shape=jax.ShapeDtypeStruct((L, W), BF16), in_s...]
    reduce_scatter x1 -> x0, waiting for transfers between devices: 89.9 us -> none  [body(): lax.psum_scatter(partial_value.astype(jnp.bfloat16), 'tensor', scatter_di...]
    psum x2 -> x0, blocking collectives: 62.8 us -> none  [the longest x1 34.3 us: body(): sums = lax.psum(jnp.sum(pooled * pooled, axis=-1), 'tensor')]
    all_gather x1 -> x0, waiting for transfers between devices: 62.4 us -> none  [body(): lax.all_gather(normed, 'tensor', axis=1, tiled=True)]
    all_to_all x1 -> x0, waiting for transfers between devices: 40.4 us -> none  [body(): lax.all_to_all(outgoing, 'req', split_axis=0, concat_axis=0, tiled=True)]
    all_to_all x1 -> x0, starting transfers between devices: 16.9 us -> none  [body(): lax.all_to_all(outgoing, 'req', split_axis=0, concat_axis=0, tiled=True)]
    dot_general x4 -> x0, matrix products: 9.21 us -> none  [the longest x1 4.65 us: body(): jnp.dot(lax.all_gather(normed, 'tensor', axis=1, tiled=True), w_flat, pre...]
    scatter x2 -> x0, local copies, waits for them, and re-layouts: 3.23 us -> none  [the longest x1 1.61 us: body(): jnp.zeros((length,), bool).at[rpos.reshape(-1)].set(True, mode='drop')]
  transfers between devices with their start and end apart: 3 -> 0, of which waited for: 3 -> 0; matrix products, arithmetic and copies ran while one was open for 3% -> 0% of each run, Pallas kernels for 0% -> 0%
where the time goes in v1:
time: 121 us
  Pallas kernels  112 us (93%)
  local copies, waits for them, and re-layouts  9.21 us (8%)
    pallas_call x1, Pallas kernels, body(): pl.pallas_call(kernel, out_shape=jax.ShapeDtypeStruct((L, W), BF16), in_s...  112 us
    unnamed x15, local copies, waits for them, and re-layouts  7.85 us

profile of v1, /device:TPU:1, one launch (start us, length us, event | category | flops | bytes accessed | tf_op | source)
XLA Modules:
  0.0 121.0 jit_solution(14946106792829713235)
XLA Ops:
  0.0 0.7 reshape.14.gv_r
  0.7 0.7 reshape.15.gd_r
  1.4 0.0 copy-start
  1.4 1.9 %copy-done = bf16[4096,3,128]{2,0,1:T(8,128)(2,1)S(1)} copy-done((bf16[4096,3,128]{2,0,1:T(8,128)(2,1)S(1)}, bf16[4096,3,128]{2,0,1:T(8,128)(2,1)}, u32[]{:S(2)}) %copy-start) | copy-done | bytes 3145752
  3.3 0.0 copy-start.1
  3.3 1.2 %copy-done.1 = bf16[128,4096]{1,0:T(8,128)(2,1)S(1)} copy-done((bf16[128,4096]{1,0:T(8,128)(2,1)S(1)}, bf16[128,4096]{1,0:T(8,128)(2,1)}, u32[]{:S(2)}) %copy-start.1) | copy-done | bytes 1048600
  4.5 0.0 copy-start.2
  4.5 1.1 copy-done.2
  5.6 0.0 copy-start.3
  5.6 0.9 copy-done.3
  6.5 0.0 copy-start.4
  6.5 0.7 copy-done.4
  7.2 0.0 copy-start.5
  7.2 0.7 copy-done.5
  7.9 0.0 copy-start.6
  7.9 0.7 copy-done.6
  8.6 111.8 %shard_map.91 = bf16[384,256]{1,0:T(8,128)(2,1)S(1)} custom-call(bf16[384,256]{1,0:T(8,128)(2,1)S(1)} %copy-done.3, bf16[6,6,32,256]{3,2,1,0:T(8,128)(2,1)S(1)} %bitcast.6, s32[2,1024]{1,0:T(2,128)S(1)} %bitcast.7, s32[1,1024]{1,0:T(1,128)S(1)} %bitcast.8, s32[1,1024]{1,0:T(1,128)S(1)} %bitcast.9, bf16[1,256]{1,0:T(2,128)(2,1)S(1)} %reshape.14.gv_r, ...), custom_call_target="tpu_custom_call" | custom-call | tf_op jit(solution)/shard_map/pallas_call | solution.py:261
  120.3 0.7 copy.11
Async XLA Ops:
  1.4 1.9 %copy-start = (bf16[4096,3,128]{2,0,1:T(8,128)(2,1)S(1)}, bf16[4096,3,128]{2,0,1:T(8,128)(2,1)}, u32[]{:S(2)}) copy-start(bf16[4096,3,128]{2,0,1:T(8,128)(2,1)} %param.16) | copy-start | bytes 9437188
  3.3 1.2 %copy-start.1 = (bf16[128,4096]{1,0:T(8,128)(2,1)S(1)}, bf16[128,4096]{1,0:T(8,128)(2,1)}, u32[]{:S(2)}) copy-start(bf16[128,4096]{1,0:T(8,128)(2,1)} %wout_h.1) | copy-start | bytes 3145732
  4.5 1.1 copy-start.2
  5.6 0.9 copy-start.3
  6.5 0.7 copy-start.4
  7.2 0.7 copy-start.5
  7.9 0.7 copy-start.6

commit v2 on v1

--- a/solution.py
+++ b/solution.py
@@ -22,6 +22,30 @@
 F32 = jnp.float32
 BF16 = jnp.bfloat16
 
+UP_A, DN_A, UP_B, DN_B = (1, 0), (-1, 0), (0, 1), (0, -1)
+BOTH_B = (UP_B, DN_B)
+AHEAD = (
+    (UP_A, DN_A, UP_B, DN_B),
+    (
+        (
+            (-1, 0, 0, (UP_A,) + BOTH_B), (1, 0, 0, BOTH_B), (0, -1, 0, (UP_B,)), (0, 1, 0, ()),
+            (1, 0, 1, (DN_A,) + BOTH_B), (-1, 0, 1, BOTH_B), (0, 1, 1, (DN_B,)), (0, -1, 1, ()),
+        ),
+        (
+            (2, 0, 0, BOTH_B), (2, 0, 1, BOTH_B),
+            (-1, -1, 0, (UP_B,)), (1, -1, 0, (UP_B,)), (-1, 1, 0, ()), (1, 1, 0, ()),
+            (-1, 1, 1, (DN_B,)), (1, 1, 1, (DN_B,)), (-1, -1, 1, ()), (1, -1, 1, ()),
+            (0, 2, 0, ()), (0, 2, 1, ()),
+        ),
+        (
+            (2, -1, 0, (UP_B,)), (2, 1, 0, ()), (2, 1, 1, (DN_B,)), (2, -1, 1, ()),
+            (-1, 2, 0, ()), (-1, 2, 1, ()), (1, 2, 0, ()), (1, 2, 1, ()),
+        ),
+        ((2, 2, 0, ()), (2, 2, 1, ())),
+    ),
+)
+SENDS = 30
+
 
 def iota(shape, dim):
     return lax.broadcasted_iota(jnp.int32, shape, dim)
@@ -38,7 +62,7 @@
 def kernel(
     text_h, patch_h, grid_r, req_r, slot_r, gv_r, gd_r, wqkv_h, wout_h, out_r,
     text_v, patch_v, w_v, wcol, stage_f, stage, recv, recv_f, place, rcat, xraw_v, xfull, cfull,
-    acc, oacc, loc_sem, w_send, w_recv, a_send, a_recv, x_send, x_recv, c_send, c_recv,
+    acc, oacc, stat, loc_sem, w_send, w_recv, a_send, a_recv, x_send, x_recv, c_send, c_recv,
 ):
     me_r = lax.axis_index("req")
     me_t = lax.axis_index("tensor")
@@ -116,20 +140,48 @@
             recv_sem=w_recv.at[me_t], device_id={"tensor": to}, device_id_type=MESH,
         )
 
-    def t_copy(buf, send, rec, d):
-        to = lax.rem(me_t + d, NT)
-        return pltpu.make_async_remote_copy(
-            src_ref=buf.at[me_t], dst_ref=buf.at[me_t], send_sem=send.at[d],
-            recv_sem=rec.at[me_t], device_id={"tensor": to}, device_id_type=MESH,
-        )
-
-    def t_wait(buf, send, rec, d):
+    def w_wait(d):
         frm = lax.rem(me_t + d, NT)
         pltpu.make_async_remote_copy(
-            src_ref=buf.at[frm], dst_ref=buf.at[frm], send_sem=send.at[d],
-            recv_sem=rec.at[frm], device_id={"tensor": frm}, device_id_type=MESH,
+            src_ref=wcol.at[frm], dst_ref=wcol.at[frm], send_sem=w_send.at[d],
+            recv_sem=w_recv.at[frm], device_id={"tensor": frm}, device_id_type=MESH,
         ).wait_recv()
-        return frm
+
+    core = lax.rem(me_r, 2)
+    tx, ty = lax.rem(me_t, 4), me_t // 4
+    pa, pb = tx + core * (ty - tx), ty + core * (tx - ty)
+    sa, sb = 1 + 3 * core, 4 - 3 * core
+
+    def at(da, db):
+        return lax.rem(pa + da + 4, 4) * sa + lax.rem(pb + db + 4, 4) * sb
+
+    def hop(buf, cut, send, rec, da, db, h, ka, kb, k):
+        t, to = at(da, db), at(ka, kb)
+        rows = pl.ds(0, cut) if h == 0 else pl.ds(cut, buf.shape[1] - cut)
+        return pltpu.make_async_remote_copy(
+            src_ref=buf.at[t, rows], dst_ref=buf.at[t, rows], send_sem=send.at[k],
+            recv_sem=rec.at[t, h], device_id={"tensor": to}, device_id_type=MESH,
+        )
+
+    def gather(buf, cut, send, rec, use):
+        sent = []
+
+        def push(da, db, h, *to):
+            for ka, kb in to:
+                copy = hop(buf, cut, send, rec, da, db, h, ka, kb, len(sent))
+                copy.start()
+                sent.append(copy)
+
+        for h in range(2):
+            push(0, 0, h, *AHEAD[0])
+        use(at(0, 0))
+        for group in AHEAD[1]:
+            for da, db, h, to in group:
+                hop(buf, cut, send, rec, da, db, h, 0, 1, 0).wait_recv()
+                push(da, db, h, *to)
+            for da, db in sorted({(g[0], g[1]) for g in group if g[2] == 1}):
+                use(at(da, db))
+        return sent
 
     def loop(lo, hi, f):
         def step(d, _):
@@ -198,23 +250,19 @@
     r8 = iota((8, W), 0)
     xfull[me_t, L:, :] = jnp.where(r8 < 4, two(s_img, r8), two(s_row, r8 - 4)).astype(BF16)
 
-    loop(1, NT, lambda d: t_copy(xfull, x_send, x_recv, d).start())
     for copy in load_w:
         copy.wait()
     load_o.wait()
+    acc[...] = jnp.zeros_like(acc)
+    stat[...] = jnp.zeros_like(stat)
 
     def project(t):
         rows = pl.ds(pl.multiple_of(t * W, W), W)
-        return dot(xfull[t, :L, :], w_v[rows, :])
-
-    acc[...] = project(me_t)
-
-    def gather_x(d, sums):
-        t = t_wait(xfull, x_send, x_recv, d)
-        acc[...] += project(t)
-        return sums + xfull[t, L:, :].astype(F32)
-
-    sums = lax.fori_loop(1, NT, gather_x, xfull[me_t, L:, :].astype(F32))
+        acc[...] += dot(xfull[t, :L, :], w_v[rows, :])
+        stat[...] += xfull[t, L:, :].astype(F32)
+
+    x_sent = gather(xfull, 200, x_send, x_recv, project)
+    sums = stat[...]
 
     def whole(r):
         return jnp.concatenate(
@@ -236,22 +284,20 @@
     expo = jnp.exp(scores - top)
     probs = (expo / jnp.sum(expo, axis=-1, keepdims=True)).astype(BF16)
     cfull[me_t] = dot(probs, qkv[:, 2 * HD:]).astype(BF16)
-    loop(1, NT, lambda d: t_copy(cfull, c_send, c_recv, d).start())
-    oacc[...] = dot(cfull[me_t], wcol[me_t])
-
-    def gather_c(d):
-        t_wait(wcol, w_send, w_recv, d)
-        t = t_wait(cfull, c_send, c_recv, d)
+    loop(1, NT, w_wait)
+    oacc[...] = jnp.zeros_like(oacc)
+
+    def combine(t):
         oacc[...] += dot(cfull[t], wcol[t])
 
-    loop(1, NT, gather_c)
+    c_sent = gather(cfull, L // 2, c_send, c_recv, combine)
     x_in = (xraw_v[...] * rv_c).astype(BF16).astype(F32)
     out_r[...] = (x_in + oacc[...]).astype(BF16)
 
     loop(1, NR, lambda d: a_copy(d).wait_send())
     loop(1, NT, lambda d: w_copy(d).wait_send())
-    loop(1, NT, lambda d: t_copy(xfull, x_send, x_recv, d).wait_send())
-    loop(1, NT, lambda d: t_copy(cfull, c_send, c_recv, d).wait_send())
+    for copy in x_sent + c_sent:
+        copy.wait_send()
 
 
 def body(text, patches, grids, image_request, slot_start, vis_gain, dec_gain, w_qkv, w_out):
@@ -279,11 +325,12 @@
             pltpu.VMEM((NT, L, HD), BF16),
             pltpu.VMEM((L, 3 * HD), F32),
             pltpu.VMEM((L, W), F32),
+            pltpu.VMEM((8, W), F32),
             dma((6,)), dma((NT,)), dma((NT,)), dma((NR,)), dma((NR,)),
-            dma((NT,)), dma((NT,)), dma((NT,)), dma((NT,)),
+            dma((SENDS,)), dma((NT, 2)), dma((SENDS,)), dma((NT, 2)),
         ],
         compiler_params=pltpu.CompilerParams(
-            collective_id=0, has_side_effects=True, vmem_limit_bytes=48 * 2**20
+            collective_id=0, has_side_effects=True, vmem_limit_bytes=62 * 2**20
         ),
     )(
         text,

time: 121 us -> 73.2 us (0.60)
  the two profiles are of different devices: /device:TPU:1 before, /device:TPU:2 now
where the time goes in v2:
time: 73.2 us; the launch traced here: 72.9 us
  Pallas kernels  68.8 us (94%)
  local copies, waits for them, and re-layouts  4.16 us (6%)
    pallas_call x1, Pallas kernels, body(): pl.pallas_call(kernel, out_shape=jax.ShapeDtypeStruct((L, W), BF16), in_s...  68.8 us
    unnamed x1, local copies, waits for them, and re-layouts  1.62 us

profile of v2, /device:TPU:2, one launch (start us, length us, event | category | flops | bytes accessed | tf_op | source)
XLA Modules:
  0.0 72.9 jit_solution(17716655643881099062)
XLA Ops:
  0.0 1.2 %reshape.14.gv_r = bf16[1,256]{1,0:T(2,128)(2,1)} reshape(bf16[256]{0:T(256)(128)(2,1)} %param.14) | data formatting | bytes 1024 | tf_op jit(solution)/shard_map/reshape | solution.py:341
  1.2 1.3 %reshape.15.gd_r = bf16[1,4096]{1,0:T(2,128)(2,1)} reshape(bf16[4096]{0:T(1024)(128)(2,1)} %param.15) | data formatting | bytes 16384 | tf_op jit(solution)/shard_map/reshape | solution.py:342
  2.5 68.8 %shard_map.91 = bf16[384,256]{1,0:T(8,128)(2,1)} custom-call(bf16[384,256]{1,0:T(8,128)(2,1)} %text_h.1, bf16[6,6,32,256]{3,2,1,0:T(8,128)(2,1)} %bitcast.6, s32[2,1024]{1,0:T(2,128)} %bitcast.7, s32[1,1024]{1,0:T(1,128)} %bitcast.8, s32[1,1024]{1,0:T(1,128)} %bitcast.9, bf16[1,256]{1,0:T(2,128)(2,1)} %reshape.14.gv_r, bf16[1,4096]{1,0:T(2,128)(2,1)} %reshape.15.gd_r, ...), custom_call_target="tpu_custom_call" | custom-call | tf_op jit(solution)/shard_map/pallas_call | solution.py:307
  71.3 1.6 %copy.11 = bf16[384,256]{1,0:T(8,128)(2,1)} copy(bf16[384,256]{1,0:T(8,128)(2,1)} %shard_map.91) | data formatting | bytes 393216

commit v3 on v1

v3 whole, which is shorter than its diff:
```python
import jax
import jax.numpy as jnp
from jax import lax
from jax.experimental import pallas as pl
from jax.experimental.pallas import tpu as pltpu
from jax.sharding import PartitionSpec as P

D = 4096
HD = 128
L = 384
W = 256
NR = 32
NZ = 16
NT = 16
IMG = 32
CELLS = 9
TEXT = L - NR * CELLS
PACK = 40
GROUP = 72
EPS = 1e-05
MESH = pl.DeviceIdType.MESH
F32 = jnp.float32
BF16 = jnp.bfloat16
X_BLOCKS = ((0, 96), (96, 72), (168, 72), (240, 72), (312, 80))
X_START = (0.0, 2.5, 4.0, 5.5, 7.0)
C_BLOCKS = ((0, 192), (192, 192))
C_START = (0.0, 0.5)
PHASES = 5


def iota(shape, dim):
    return lax.broadcasted_iota(jnp.int32, shape, dim)


def dot(a, b):
    return lax.dot_general(a, b, (((1,), (0,)), ((), ())), preferred_element_type=F32)


def dot_nt(a, b):
    return lax.dot_general(a, b, (((1,), (1,)), ((), ())), preferred_element_type=F32)


def shift_of(e):
    return (e + 1) // 2 if e % 2 else -(e // 2)


def mirror(e):
    return e if e in (0, NZ - 1) else (e + 1 if e % 2 else e - 1)


def order(starts):
    keys = [(start + p, b, p) for b, start in enumerate(starts) for p in range(PHASES)]
    return [(b, p) for _, b, p in sorted(keys)]


def cell_of(n):
    e = (n * 3641) >> 16
    q = n - 18 * e
    s = (q >= CELLS).astype(jnp.int32)
    c = q - CELLS * s
    i = (c >= 3).astype(jnp.int32) + (c >= 6).astype(jnp.int32)
    return e, s, c.astype(F32), i.astype(F32), (c - 3 * i).astype(F32)


def place_of(start, hh, hw, c, i, j):
    valid = (i < hh) & (j < hw)
    before = jnp.minimum(i, hh) * hw + jnp.where(i < hh, jnp.minimum(j, hw), 0.0)
    return start + jnp.where(valid, i * hw + j, hh * hw + c - before), valid


def kernel(
    text_h, patch_h, grid_r, req_r, slot_r, gv_r, gd_r, wqkv_h, wout_h, out_r,
    text_v, patch_v, w_v, wcol, pool, stage_f, stage, recv, to_slot, to_pos, xraw, sq_i, sq_r,
    xfull, cfull, acc, oacc, stat, loc_sem, p_sem, w_send, w_recv, a_send, a_recv,
    x_send, x_recv, c_send, c_recv,
):
    me_r = lax.axis_index("req")
    me_t = lax.axis_index("tensor")
    core = lax.rem(me_r, 2)
    me_z = me_r // 2
    sibling = me_r + 1 - 2 * core
    tx, ty = lax.rem(me_t, 4), me_t // 4
    pa, pb = tx + core * (ty - tx), ty + core * (tx - ty)
    sa, sb = 1 + 3 * core, 4 - 3 * core

    def at(da, db):
        return lax.rem(pa + da + 4, 4) * sa + lax.rem(pb + db + 4, 4) * sb

    def z_peer(shift):
        return lax.rem(me_z + shift + NZ, NZ) * 2 + core

    half = pl.ds(pl.multiple_of(core * (HD // 2), HD // 2), HD // 2)

    def w_cols(t):
        return pl.ds(pl.multiple_of(t * W, W), W)

    load_p = pltpu.make_async_copy(patch_h, patch_v, loc_sem.at[0])
    load_t = pltpu.make_async_copy(text_h, text_v, loc_sem.at[1])
    load_w = [
        pltpu.make_async_copy(wqkv_h.at[j], w_v.at[:, pl.ds(j * HD, HD)], loc_sem.at[2 + j])
        for j in range(3)
    ]
    load_o = pltpu.make_async_copy(
        wout_h.at[half, w_cols(me_t)], wcol.at[me_t, half], loc_sem.at[5]
    )
    load_p.start()
    barrier = pltpu.get_barrier_semaphore()

    def greet(**device):
        pl.semaphore_signal(barrier, inc=1, device_id=device, device_id_type=MESH)

    for e in range(NZ - 1, 0, -1):
        greet(req=z_peer(shift_of(e)))
    greet(req=sibling)
    for d in range(1, NT):
        greet(tensor=lax.rem(me_t + d, NT))
    load_t.start()
    load_o.start()
    for copy in load_w:
        copy.start()

    req = req_r[...]
    req8 = jnp.broadcast_to(req.astype(F32), (8, NR * IMG)).astype(BF16)
    ours = (
        iota((2 * IMG, NR * IMG), 1) == me_z * 2 * IMG + iota((2 * IMG, NR * IMG), 0)
    ).astype(BF16)
    goes = dot_nt(req8, ours)[0:1, :]
    row_s = (iota((NR, 2 * IMG), 0) >= NZ).astype(jnp.int32)
    col_s = (iota((NR, 2 * IMG), 1) >= IMG).astype(jnp.int32)
    wanted = ((iota((NR, 2 * IMG), 0) - NZ * row_s) * 2 + core).astype(F32)
    pick = ((row_s == col_s) & (wanted == goes)).astype(BF16)

    load_p.wait()
    for c in range(CELLS):
        i, j = 2 * (c // 3), 2 * (c % 3)
        total = (
            patch_v[i, j].astype(F32) + patch_v[i, j + 1].astype(F32)
            + patch_v[i + 1, j].astype(F32) + patch_v[i + 1, j + 1].astype(F32)
        )
        pool[c, core] = (total * 0.25).astype(BF16)
    stage_f[...] = jnp.zeros_like(stage_f)

    pl.semaphore_wait(barrier, NZ - 1 + 1 + NT - 1)

    swap = pltpu.make_async_remote_copy(
        src_ref=pool.at[:, core], dst_ref=pool.at[:, core], send_sem=p_sem.at[0],
        recv_sem=p_sem.at[1], device_id={"req": sibling}, device_id_type=MESH,
    )
    swap.start()
    swap.wait_recv()
    for c in range(CELLS):
        sent = dot(pick, pool[c].reshape(2 * IMG, W))
        for s in range(2):
            rows = sent[s * NZ:(s + 1) * NZ]
            stage_f[pl.ds(s * CELLS + c, NZ, stride=PACK), :] = rows[:, :HD]
            stage_f[pl.ds((2 + s) * CELLS + c, NZ, stride=PACK), :] = rows[:, HD:]
    stage[...] = stage_f[...].astype(BF16).reshape(NZ, PACK, HD)

    def packet(e):
        to = lax.rem(me_z + shift_of(e) + NZ, NZ)
        return pltpu.make_async_remote_copy(
            src_ref=stage.at[to], dst_ref=recv.at[mirror(e)], send_sem=a_send.at[e],
            recv_sem=a_recv.at[mirror(e)], device_id={"req": to * 2 + core}, device_id_type=MESH,
        )

    for e in range(NZ - 1, 0, -1):
        packet(e).start()
    recv[0] = stage[me_z]

    row = iota((8, NR * IMG), 0)
    start = jnp.broadcast_to(slot_r[...], (8, NR * IMG))
    half_h = jnp.broadcast_to(grid_r[0:1, :], (8, NR * IMG)) >> 1
    half_w = jnp.broadcast_to(grid_r[1:2, :], (8, NR * IMG)) >> 1
    facts = jnp.where(
        row == 0, start >> 4, jnp.where(row == 1, start & 15, jnp.where(row == 2, half_h, half_w))
    )
    facts = jnp.where(jnp.broadcast_to(req, (8, NR * IMG)) == me_r, facts, 0).astype(F32).astype(BF16)
    seg = ((iota((NR, NR * IMG), 1) >> 5) == iota((NR, NR * IMG), 0)).astype(BF16)
    by_src = dot_nt(facts, seg).astype(BF16)
    src_col = dot_nt(seg, facts)
    start_c = src_col[:, 0:1] * 16.0 + src_col[:, 1:2]
    off = iota((NR, L), 1).astype(F32) - start_c
    free = 1.0 - jnp.max(((off >= 0.0) & (off < float(CELLS))).astype(F32), axis=0, keepdims=True)
    earlier = (iota((L, L), 0) < iota((L, L), 1)).astype(BF16)
    rank = dot(jnp.broadcast_to(free, (8, L)).astype(BF16), earlier)[0:1, :]
    place = iota((L, L), 1)
    rest = (iota((L, L), 0).astype(F32) == jnp.where(free > 0.5, rank, -1.0)).astype(F32)

    n_col = iota((L, 1), 0) - TEXT
    n_row = iota((1, L), 1) - TEXT

    def source(n):
        e, s, c, i, j = cell_of(n)
        mag = (e + 1) >> 1
        z = (me_z + NZ + jnp.where((e & 1) == 1, mag, -mag)) & (NZ - 1)
        return jnp.where(n >= 0, 2 * z + s, -1), c, i, j

    k_col, c_c, i_c, j_c = source(n_col)
    _, c_r, i_r, j_r = source(n_row)
    expand = (k_col == iota((L, NR), 1)).astype(BF16)
    f_col = dot_nt(expand, by_src)
    f_row = dot_nt(by_src, expand)
    pos_c, valid_c = place_of(
        f_col[:, 0:1] * 16.0 + f_col[:, 1:2], f_col[:, 2:3], f_col[:, 3:4], c_c, i_c, j_c
    )
    pos_r, valid_r = place_of(
        f_row[0:1] * 16.0 + f_row[1:2], f_row[2:3], f_row[3:4], c_r, i_r, j_r
    )
    pos_c = jnp.where(n_col >= 0, pos_c, -1.0)
    to_slot[...] = (rest + (place.astype(F32) == pos_c).astype(F32)).astype(BF16)
    p8 = iota((8, L), 1)
    digits = jnp.where(iota((8, L), 0) == 0, p8 >> 4, p8 & 15).astype(F32).astype(BF16)
    rest_r = dot_nt(digits, rest.astype(BF16))
    pos_r = jnp.where(n_row >= 0, pos_r, rest_r[0:1] * 16.0 + rest_r[1:2])
    is_img_r = (n_row >= 0) & valid_r
    bad_r = ((n_row >= 0) & jnp.logical_not(valid_r)).astype(F32)

    gv2 = gv_r[...].astype(F32)
    gv = jnp.concatenate([gv2[0:1], gv2[1:2]], axis=1)
    gd2 = gd_r[...].astype(F32)
    gd_i = iota((D // HD, HD), 0)
    gd = jnp.concatenate(
        [jnp.sum(jnp.where(gd_i == 2 * me_t + h, gd2, 0.0), axis=0, keepdims=True) for h in range(2)],
        axis=1,
    )
    load_t.wait()
    xraw[...] = dot(to_slot[...], text_v[...])

    sel_r, sel_c = iota((GROUP, 4 * PACK), 0), iota((GROUP, 4 * PACK), 1)
    sel_e = (sel_r * 3641) >> 16
    sel_at = sel_e * PACK + sel_r - 18 * sel_e
    left = (sel_c == sel_at).astype(BF16)
    right = (sel_c == sel_at + 18).astype(BF16)

    def two(s, r):
        hi = s.astype(BF16).astype(F32)
        lo = s - hi

        def wide(v):
            return jnp.concatenate([v[:, W:], jnp.zeros((8, 2 * W - L), F32)], axis=1)

        return jnp.where(
            r == 0, hi[:, :W], jnp.where(r == 1, wide(hi), jnp.where(r == 2, lo[:, :W], wide(lo)))
        )

    def fill(b):
        if b == 0:
            x = xraw[:TEXT]
            rows = slice(0, TEXT)
            sq_i[rows] = jnp.zeros((TEXT, W), BF16)
        else:
            for e in range(4 * (b - 1), 4 * b):
                if e:
                    packet(mirror(e)).wait_recv()
            rows = slice(TEXT + GROUP * (b - 1), TEXT + GROUP * b)
            got = recv[4 * (b - 1):4 * b].reshape(4 * PACK, HD)
            img = jnp.concatenate([dot(left, got), dot(right, got)], axis=1)
            x = jnp.where(valid_c[rows], img * gv, xraw[rows])
            xraw[rows] = x
            sq_i[rows] = (img * img).astype(BF16)
        xfull[me_t, rows] = (x * gd).astype(BF16)
        sq_r[rows] = (x * x).astype(BF16)
        if b == len(X_BLOCKS) - 1:
            ones = jnp.ones((8, W), BF16)
            r8 = iota((8, W), 0)
            xfull[me_t, L:] = jnp.where(
                r8 < 4, two(dot_nt(ones, sq_i[...]), r8), two(dot_nt(ones, sq_r[...]), r8 - 4)
            ).astype(BF16)

    def gather(buf, blocks, starts, send, rec, fill, use):
        sent = []

        def copy(da, db, b, ka, kb, k):
            t = at(da, db)
            rows = pl.ds(*blocks[b])
            return pltpu.make_async_remote_copy(
                src_ref=buf.at[t, rows], dst_ref=buf.at[t, rows], send_sem=send.at[k],
                recv_sem=rec.at[t, b], device_id={"tensor": at(ka, kb)}, device_id_type=MESH,
            )

        def push(da, db, b, ka, kb):
            one = copy(da, db, b, ka, kb, len(sent))
            one.start()
            sent.append(one)

        def wait(da, db, b):
            copy(da, db, b, 0, 1, 0).wait_recv()

        def turn(column, b):
            return 1 - 2 * lax.rem(pb + column + b, 2)

        def both(da, b):
            push(da, 0, b, 0, 1)
            push(da, 0, b, 0, -1)

        def around(da, b):
            wait(da, -1, b)
            wait(da, 1, b)
            s = turn(pa + da + 4, b)
            push(da, -s, b, 0, s)

        for b, p in order(starts):
            if p == 0:
                fill(b)
                push(0, 0, b, 1, 0)
                push(0, 0, b, -1, 0)
                both(0, b)
                new = ((0, 0),)
            elif p == 1:
                wait(-1, 0, b)
                wait(1, 0, b)
                s = turn(pa, b)
                push(-s, 0, b, s, 0)
                both(-1, b)
                both(1, b)
                around(0, b)
                new = ((-1, 0), (1, 0), (0, -1), (0, 1))
            elif p == 2:
                wait(2, 0, b)
                both(2, b)
                around(-1, b)
                around(1, b)
                wait(0, 2, b)
                new = ((2, 0), (-1, -1), (-1, 1), (1, -1), (1, 1), (0, 2))
            elif p == 3:
                around(2, b)
                wait(-1, 2, b)
                wait(1, 2, b)
                new = ((2, -1), (2, 1), (-1, 2), (1, 2))
            else:
                wait(2, 2, b)
                new = ((2, 2),)
            use(b, p, [at(*one) for one in new])
        return sent

    def w_copy(d):
        to = lax.rem(me_t + d, NT)
        return pltpu.make_async_remote_copy(
            src_ref=wout_h.at[half, w_cols(to)], dst_ref=wcol.at[me_t, half],
            send_sem=w_send.at[d], recv_sem=w_recv.at[me_t], device_id={"tensor": to},
            device_id_type=MESH,
        )

    def w_wait(d):
        frm = lax.rem(me_t + d, NT)
        pltpu.make_async_remote_copy(
            src_ref=wcol.at[frm, half], dst_ref=wcol.at[frm, half], send_sem=w_send.at[d],
            recv_sem=w_recv.at[frm], device_id={"tensor": frm}, device_id_type=MESH,
        ).wait_recv()

    w_swap = pltpu.make_async_remote_copy(
        src_ref=wcol.at[:, half], dst_ref=wcol.at[:, half], send_sem=p_sem.at[2],
        recv_sem=p_sem.at[3], device_id={"req": sibling}, device_id_type=MESH,
    )
    last = len(X_BLOCKS) - 1
    early = X_BLOCKS[last][0]

    def project(b, p, chunks):
        if b == 0 and p == 0:
            for d in range(1, NT):
                w_copy(d).start()
            for one in load_w:
                one.wait()
            acc[...] = jnp.zeros_like(acc)
            stat[...] = jnp.zeros_like(stat)
            row = iota((L, L), 0).astype(F32)
            to_pos[...] = (row == pos_r).astype(BF16)
        if b == last and p == 0:
            load_o.wait()
            for d in range(1, NT):
                w_wait(d)
            w_swap.start()
        for t in chunks:
            w_rows = pl.ds(pl.multiple_of(t * W, W), W)
            if b == last - 1:
                acc[:early] += dot(xfull[t, :early], w_v[w_rows, :])
            if b == last:
                acc[early:] += dot(xfull[t, early:L], w_v[w_rows, :])
                stat[...] += xfull[t, L:].astype(F32)

    x_sent = gather(xfull, X_BLOCKS, X_START, x_send, x_recv, fill, project)

    sums = stat[...]

    def whole(r):
        return jnp.concatenate(
            [sums[r:r + 1, :] + sums[r + 2:r + 3, :],
             sums[r + 1:r + 2, :L - W] + sums[r + 3:r + 4, :L - W]], axis=1
        )

    rv = jnp.where(is_img_r, lax.rsqrt(whole(0) / D + EPS), 1.0)
    rd = lax.rsqrt(rv * rv * whole(4) / D + EPS)
    cols = jnp.transpose(jnp.where(iota((8, L), 0) == 0, rv * rd, rv))
    qkv = (acc[...] * cols[:, 0:1]).astype(BF16)
    queries = dot(to_pos[...], qkv[:, :HD]).astype(BF16)

    def attend(b):
        rows = slice(C_BLOCKS[b][0], C_BLOCKS[b][0] + C_BLOCKS[b][1])
        scores = dot_nt(queries[rows], qkv[:, HD:2 * HD]) * (HD ** -0.5)
        at_q = (iota((C_BLOCKS[b][1], L), 0) + C_BLOCKS[b][0]).astype(F32)
        scores = jnp.where((at_q >= pos_r) & (bad_r < 0.5), scores, -1e30)
        expo = jnp.exp(scores - jnp.max(scores, axis=-1, keepdims=True))
        probs = (expo / jnp.sum(expo, axis=-1, keepdims=True)).astype(BF16)
        cfull[me_t, rows] = dot(probs, qkv[:, 2 * HD:]).astype(BF16)

    def combine(b, p, chunks):
        if b == 1 and p == 0:
            x_in = (xraw[...] * cols[:, 1:2]).astype(BF16)
            oacc[...] = dot(to_pos[...], x_in)
            w_swap.wait_recv()
        if b == 1:
            for t in chunks:
                oacc[...] += dot(cfull[t], wcol[t])

    c_sent = gather(cfull, C_BLOCKS, C_START, c_send, c_recv, attend, combine)
    out_r[...] = oacc[...].astype(BF16)

    swap.wait_send()
    w_swap.wait_send()
    for e in range(1, NZ):
        packet(e).wait_send()
    for d in range(1, NT):
        w_copy(d).wait_send()
    for one in x_sent + c_sent:
        one.wait_send()


def body(text, patches, grids, image_request, slot_start, vis_gain, dec_gain, w_qkv, w_out):
    vmem = pl.BlockSpec(memory_space=pltpu.VMEM)
    hbm = pl.BlockSpec(memory_space=pl.ANY)
    dma = pltpu.SemaphoreType.DMA
    return pl.pallas_call(
        kernel,
        out_shape=jax.ShapeDtypeStruct((L, W), BF16),
        in_specs=[hbm, hbm, vmem, vmem, vmem, vmem, vmem, hbm, hbm],
        out_specs=vmem,
        scratch_shapes=[
            pltpu.VMEM((L, W), BF16),
            pltpu.VMEM((6, 6, IMG, W), BF16),
            pltpu.VMEM((D, 3 * HD), BF16),
            pltpu.VMEM((NT, HD, W), BF16),
            pltpu.VMEM((CELLS, 2, IMG, W), BF16),
            pltpu.VMEM((NZ * PACK, HD), F32),
            pltpu.VMEM((NZ, PACK, HD), BF16),
            pltpu.VMEM((NZ, PACK, HD), BF16),
            pltpu.VMEM((L, L), BF16),
            pltpu.VMEM((L, L), BF16),
            pltpu.VMEM((L, W), F32),
            pltpu.VMEM((L, W), BF16),
            pltpu.VMEM((L, W), BF16),
            pltpu.VMEM((NT, L + 8, W), BF16),
            pltpu.VMEM((NT, L, HD), BF16),
            pltpu.VMEM((L, 3 * HD), F32),
            pltpu.VMEM((L, W), F32),
            pltpu.VMEM((8, W), F32),
            dma((6,)), dma((4,)), dma((NT,)), dma((NT,)), dma((NZ,)), dma((NZ,)),
            dma((15 * len(X_BLOCKS),)), dma((NT, len(X_BLOCKS))),
            dma((15 * len(C_BLOCKS),)), dma((NT, len(C_BLOCKS))),
        ],
        compiler_params=pltpu.CompilerParams(
            collective_id=0, has_side_effects=True, vmem_limit_bytes=62 * 2**20
        ),
    )(
        text,
        patches.transpose(1, 2, 0, 3),
        grids.T,
        image_request.reshape(1, -1),
        slot_start.reshape(1, -1),
        vis_gain.reshape(-1, HD),
        dec_gain.reshape(-1, HD),
        w_qkv.transpose(1, 0, 2),
        w_out,
    )


def solution(mesh):
    in_specs = (
        P("req", "tensor"),
        P("req", None, None, "tensor"),
        P(),
        P(),
        P(),
        P("tensor"),
        P(),
        P(None, None, "tensor"),
        P("tensor", None),
    )
    return jax.shard_map(
        body, mesh=mesh, in_specs=in_specs, out_specs=P("req", "tensor"), check_vma=False
    )
```

time: 121 us -> 84.4 us (0.70)
  the two profiles are of different devices: /device:TPU:1 before, /device:TPU:8 now
where the time goes in v3:
time: 84.4 us; the launch traced here: 84.3 us
  Pallas kernels  82.6 us (98%)
  local copies, waits for them, and re-layouts  1.62 us (2%)
    pallas_call x1, Pallas kernels, body(): pl.pallas_call(kernel, out_shape=jax.ShapeDtypeStruct((L, W), BF16), in_s...  82.6 us

profile of v3, /device:TPU:8, one launch (start us, length us, event | category | flops | bytes accessed | tf_op | source)
XLA Modules:
  0.0 84.3 jit_solution(3991394705994477987)
XLA Ops:
  0.0 82.6 %shard_map.91 = bf16[384,256]{1,0:T(8,128)(2,1)} custom-call(bf16[384,256]{1,0:T(8,128)(2,1)} %text_h.1, bf16[6,6,32,256]{3,2,1,0:T(8,128)(2,1)} %bitcast.8, s32[2,1024]{1,0:T(2,128)} %bitcast.9, s32[1,1024]{1,0:T(1,128)} %bitcast.11, s32[1,1024]{1,0:T(1,128)} %bitcast.12, bf16[2,128]{1,0:T(2,128)(2,1)} %bitcast.13, bf16[32,128]{1,0:T(8,128)(2,1)} %bitcast.10, ...), custom_call_target="tpu_custom_call" | custom-call | tf_op jit(solution)/shard_map/pallas_call | solution.py:432
  82.6 1.6 %copy.11 = bf16[384,256]{1,0:T(8,128)(2,1)} copy(bf16[384,256]{1,0:T(8,128)(2,1)} %shard_map.91) | data formatting | bytes 393216

commit v4 on v3

v4 whole, which is shorter than its diff:
```python
import jax
import jax.numpy as jnp
from jax import lax
from jax.experimental import pallas as pl
from jax.experimental.pallas import tpu as pltpu
from jax.sharding import PartitionSpec as P

D = 4096
HD = 128
L = 384
W = 256
NR = 32
NZ = 16
NT = 16
IMG = 32
CELLS = 9
TEXT = L - NR * CELLS
PACK = 40
GROUP = 72
EPS = 1e-05
MESH = pl.DeviceIdType.MESH
F32 = jnp.float32
BF16 = jnp.bfloat16
EARLY, SPLIT = TEXT, TEXT + 2 * GROUP
X_PARTS = ((0, EARLY), (EARLY, SPLIT - EARLY), (SPLIT, L + 8 - SPLIT))
Q_PARTS = ((0, L // 2), (L // 2, L // 2))
PEERS = (2, 1, -1)


def iota(shape, dim):
    return lax.broadcasted_iota(jnp.int32, shape, dim)


def dot(a, b):
    return lax.dot_general(a, b, (((1,), (0,)), ((), ())), preferred_element_type=F32)


def dot_nt(a, b):
    return lax.dot_general(a, b, (((1,), (1,)), ((), ())), preferred_element_type=F32)


def shift_of(e):
    return (e + 1) // 2 if e % 2 else -(e // 2)


def mirror(e):
    return e if e in (0, NZ - 1) else (e + 1 if e % 2 else e - 1)


def cell_of(n):
    e = (n * 3641) >> 16
    q = n - 18 * e
    s = (q >= CELLS).astype(jnp.int32)
    c = q - CELLS * s
    i = (c >= 3).astype(jnp.int32) + (c >= 6).astype(jnp.int32)
    return e, s, c.astype(F32), i.astype(F32), (c - 3 * i).astype(F32)


def place_of(start, hh, hw, c, i, j):
    valid = (i < hh) & (j < hw)
    before = jnp.minimum(i, hh) * hw + jnp.where(i < hh, jnp.minimum(j, hw), 0.0)
    return start + jnp.where(valid, i * hw + j, hh * hw + c - before), valid


def kernel(
    text_h, patch_h, grid_r, req_r, slot_r, gv_r, gd_r, wqkv_h, wout_h, out_r,
    text_v, patch_v, w_v, w_blk, pool, stage_f, stage, recv, to_slot, to_pos, xraw, sq_i, sq_r,
    xfull, ctx, part, part_in, acc, oacc, stat, loc_sem, p_sem, w_send, w_recv, a_send, a_recv,
    x_send, x_recv, c_send, c_recv, o_send, o_recv,
):
    me_r = lax.axis_index("req")
    me_t = lax.axis_index("tensor")
    core = me_r & 1
    me_z = me_r >> 1
    sibling = me_r + 1 - 2 * core
    tx, ty = me_t & 3, me_t >> 2
    pa, pb = tx + core * (ty - tx), ty + core * (tx - ty)
    sa, sb = 1 + 3 * core, 4 - 3 * core
    ids = {
        (da, db): ((pa + da) & 3) * sa + ((pb + db) & 3) * sb for da in range(4) for db in range(4)
    }

    def at(da, db):
        return ids[da % 4, db % 4]

    def z_peer(shift):
        return ((me_z + shift + NZ) & (NZ - 1)) * 2 + core

    def w_cols(t):
        return pl.ds(pl.multiple_of(t * W, W), W)

    heads = pl.ds(pl.multiple_of(pa * HD, HD), HD)

    load_p = pltpu.make_async_copy(patch_h, patch_v, loc_sem.at[0])
    load_t = pltpu.make_async_copy(text_h, text_v, loc_sem.at[1])
    load_w = [
        pltpu.make_async_copy(wqkv_h.at[j], w_v.at[:, pl.ds(j * HD, HD)], loc_sem.at[2 + j])
        for j in range(3)
    ]
    load_o = [
        pltpu.make_async_copy(
            wout_h.at[:, w_cols(at(0, db))], w_blk.at[(pb + db) & 3, heads], loc_sem.at[5 + db]
        )
        for db in range(4)
    ]
    load_p.start()
    barrier = pltpu.get_barrier_semaphore()

    def greet(**device):
        pl.semaphore_signal(barrier, inc=1, device_id=device, device_id_type=MESH)

    for e in range(NZ - 1, 0, -1):
        greet(req=z_peer(shift_of(e)))
    greet(req=sibling)
    for d in PEERS:
        greet(tensor=at(d, 0))
        greet(tensor=at(0, d))
    load_t.start()
    for copy in load_o + load_w:
        copy.start()

    req = req_r[...]
    req8 = jnp.broadcast_to(req.astype(F32), (8, NR * IMG)).astype(BF16)
    ours = (
        iota((2 * IMG, NR * IMG), 1) == me_z * 2 * IMG + iota((2 * IMG, NR * IMG), 0)
    ).astype(BF16)
    goes = dot_nt(req8, ours)[0:1, :]
    row_s = (iota((NR, 2 * IMG), 0) >= NZ).astype(jnp.int32)
    col_s = (iota((NR, 2 * IMG), 1) >= IMG).astype(jnp.int32)
    wanted = ((iota((NR, 2 * IMG), 0) - NZ * row_s) * 2 + core).astype(F32)
    pick = ((row_s == col_s) & (wanted == goes)).astype(BF16)

    load_p.wait()
    for c in range(CELLS):
        i, j = 2 * (c // 3), 2 * (c % 3)
        total = (
            patch_v[i, j].astype(F32) + patch_v[i, j + 1].astype(F32)
            + patch_v[i + 1, j].astype(F32) + patch_v[i + 1, j + 1].astype(F32)
        )
        pool[c, core] = (total * 0.25).astype(BF16)
    stage_f[...] = jnp.zeros_like(stage_f)

    pl.semaphore_wait(barrier, NZ - 1 + 1 + 2 * len(PEERS))

    swap = pltpu.make_async_remote_copy(
        src_ref=pool.at[:, core], dst_ref=pool.at[:, core], send_sem=p_sem.at[0],
        recv_sem=p_sem.at[1], device_id={"req": sibling}, device_id_type=MESH,
    )
    swap.start()
    swap.wait_recv()
    for c in range(CELLS):
        sent = dot(pick, pool[c].reshape(2 * IMG, W))
        for s in range(2):
            rows = sent[s * NZ:(s + 1) * NZ]
            stage_f[pl.ds(s * CELLS + c, NZ, stride=PACK), :] = rows[:, :HD]
            stage_f[pl.ds((2 + s) * CELLS + c, NZ, stride=PACK), :] = rows[:, HD:]
    stage[...] = stage_f[...].astype(BF16).reshape(NZ, PACK, HD)

    def packet(e):
        to = (me_z + shift_of(e) + NZ) & (NZ - 1)
        return pltpu.make_async_remote_copy(
            src_ref=stage.at[to], dst_ref=recv.at[mirror(e)], send_sem=a_send.at[e],
            recv_sem=a_recv.at[mirror(e)], device_id={"req": to * 2 + core}, device_id_type=MESH,
        )

    for e in range(NZ - 1, 0, -1):
        packet(e).start()
    recv[0] = stage[me_z]

    row = iota((8, NR * IMG), 0)
    start = jnp.broadcast_to(slot_r[...], (8, NR * IMG))
    half_h = jnp.broadcast_to(grid_r[0:1, :], (8, NR * IMG)) >> 1
    half_w = jnp.broadcast_to(grid_r[1:2, :], (8, NR * IMG)) >> 1
    facts = jnp.where(
        row == 0, start >> 4, jnp.where(row == 1, start & 15, jnp.where(row == 2, half_h, half_w))
    )
    facts = jnp.where(jnp.broadcast_to(req, (8, NR * IMG)) == me_r, facts, 0).astype(F32).astype(BF16)
    seg = ((iota((NR, NR * IMG), 1) >> 5) == iota((NR, NR * IMG), 0)).astype(BF16)
    by_src = dot_nt(facts, seg).astype(BF16)
    src_col = dot_nt(seg, facts)
    start_c = src_col[:, 0:1] * 16.0 + src_col[:, 1:2]
    off = iota((NR, L), 1).astype(F32) - start_c
    free = 1.0 - jnp.max(((off >= 0.0) & (off < float(CELLS))).astype(F32), axis=0, keepdims=True)
    earlier = (iota((L, L), 0) < iota((L, L), 1)).astype(BF16)
    rank = dot(jnp.broadcast_to(free, (8, L)).astype(BF16), earlier)[0:1, :]
    place = iota((L, L), 1)
    rest = (iota((L, L), 0).astype(F32) == jnp.where(free > 0.5, rank, -1.0)).astype(F32)

    n_col = iota((L, 1), 0) - TEXT
    n_row = iota((1, L), 1) - TEXT

    def source(n):
        e, s, c, i, j = cell_of(n)
        mag = (e + 1) >> 1
        z = (me_z + NZ + jnp.where((e & 1) == 1, mag, -mag)) & (NZ - 1)
        return jnp.where(n >= 0, 2 * z + s, -1), c, i, j

    k_col, c_c, i_c, j_c = source(n_col)
    _, c_r, i_r, j_r = source(n_row)
    expand = (k_col == iota((L, NR), 1)).astype(BF16)
    f_col = dot_nt(expand, by_src)
    f_row = dot_nt(by_src, expand)
    pos_c, valid_c = place_of(
        f_col[:, 0:1] * 16.0 + f_col[:, 1:2], f_col[:, 2:3], f_col[:, 3:4], c_c, i_c, j_c
    )
    pos_r, valid_r = place_of(
        f_row[0:1] * 16.0 + f_row[1:2], f_row[2:3], f_row[3:4], c_r, i_r, j_r
    )
    pos_c = jnp.where(n_col >= 0, pos_c, -1.0)
    to_slot[...] = (rest + (place.astype(F32) == pos_c).astype(F32)).astype(BF16)
    p8 = iota((8, L), 1)
    digits = jnp.where(iota((8, L), 0) == 0, p8 >> 4, p8 & 15).astype(F32).astype(BF16)
    rest_r = dot_nt(digits, rest.astype(BF16))
    pos_r = jnp.where(n_row >= 0, pos_r, rest_r[0:1] * 16.0 + rest_r[1:2])
    is_img_r = (n_row >= 0) & valid_r
    bad_r = ((n_row >= 0) & jnp.logical_not(valid_r)).astype(F32)

    gv2 = gv_r[...].astype(F32)
    gv = jnp.concatenate([gv2[0:1], gv2[1:2]], axis=1)
    gd2 = gd_r[...].astype(F32)
    gd_i = iota((D // HD, HD), 0)
    gd = jnp.concatenate(
        [jnp.sum(jnp.where(gd_i == 2 * me_t + h, gd2, 0.0), axis=0, keepdims=True) for h in range(2)],
        axis=1,
    )
    load_t.wait()
    xraw[...] = dot(to_slot[...], text_v[...])

    sel_r, sel_c = iota((GROUP, 4 * PACK), 0), iota((GROUP, 4 * PACK), 1)
    sel_e = (sel_r * 3641) >> 16
    sel_at = sel_e * PACK + sel_r - 18 * sel_e
    left = (sel_c == sel_at).astype(BF16)
    right = (sel_c == sel_at + 18).astype(BF16)

    def two(s, r):
        hi = s.astype(BF16).astype(F32)
        lo = s - hi

        def wide(v):
            return jnp.concatenate([v[:, W:], jnp.zeros((8, 2 * W - L), F32)], axis=1)

        return jnp.where(
            r == 0, hi[:, :W], jnp.where(r == 1, wide(hi), jnp.where(r == 2, lo[:, :W], wide(lo)))
        )

    def put(x, rows):
        xfull[me_t, rows] = (x * gd).astype(BF16)
        sq_r[rows] = (x * x).astype(BF16)

    def fill(g):
        for e in range(4 * g, 4 * g + 4):
            if e:
                packet(mirror(e)).wait_recv()
        rows = slice(TEXT + GROUP * g, TEXT + GROUP * (g + 1))
        got = recv[4 * g:4 * g + 4].reshape(4 * PACK, HD)
        img = jnp.concatenate([dot(left, got), dot(right, got)], axis=1)
        x = jnp.where(valid_c[rows], img * gv, xraw[rows])
        xraw[rows] = x
        sq_i[rows] = (img * img).astype(BF16)
        put(x, rows)

    sent = []

    def x_copy(da, db, h, ka, kb, k):
        t = at(da, db)
        rows = pl.ds(*X_PARTS[h])
        return pltpu.make_async_remote_copy(
            src_ref=xfull.at[t, rows], dst_ref=xfull.at[t, rows], send_sem=x_send.at[k],
            recv_sem=x_recv.at[t, h], device_id={"tensor": at(ka, kb)}, device_id_type=MESH,
        )

    def push(da, db, h, *to):
        for ka, kb in to:
            one = x_copy(da, db, h, ka, kb, len(sent))
            one.start()
            sent.append(one)

    def wait(da, db, h):
        x_copy(da, db, h, 0, 1, 0).wait_recv()

    def w_copy(i, db):
        return pltpu.make_async_remote_copy(
            src_ref=wout_h.at[:, w_cols(at(PEERS[i], db))], dst_ref=w_blk.at[(pb + db) & 3, heads],
            send_sem=w_send.at[i, db], recv_sem=w_recv.at[i, db],
            device_id={"tensor": at(PEERS[i], 0)}, device_id_type=MESH,
        )

    def w_wait(i, db):
        rows = pl.ds(pl.multiple_of(((pa - PEERS[i]) & 3) * HD, HD), HD)
        block = w_blk.at[(pb + db) & 3, rows]
        pltpu.make_async_remote_copy(
            src_ref=block, dst_ref=block, send_sem=w_send.at[i, db], recv_sem=w_recv.at[i, db],
            device_id={"tensor": at(-PEERS[i], 0)}, device_id_type=MESH,
        ).wait_recv()

    sq_i[:TEXT] = jnp.zeros((TEXT, W), BF16)
    put(xraw[:TEXT], slice(0, TEXT))
    ring_b = tuple((0, d) for d in PEERS)
    push(0, 0, 0, *((d, 0) for d in PEERS), *ring_b)
    for i in range(len(PEERS)):
        for db in range(4):
            w_copy(i, db).start()
    to_pos[...] = (iota((L, L), 0).astype(F32) == pos_r).astype(BF16)
    stat[...] = jnp.zeros_like(stat)
    acc[...] = jnp.zeros_like(acc)
    for da in PEERS[::-1]:
        wait(da, 0, 0)
        push(da, 0, 0, *ring_b)

    up_a, dn_a, up_b, dn_b = (1, 0), (-1, 0), (0, 1), (0, -1)
    fill(0)
    fill(1)
    push(0, 0, 1, up_a, dn_a, up_b, dn_b)
    fill(2)
    fill(3)
    ones = jnp.ones((8, W), BF16)
    r8 = iota((8, W), 0)
    xfull[me_t, L:] = jnp.where(
        r8 < 4, two(dot_nt(ones, sq_i[...]), r8), two(dot_nt(ones, sq_r[...]), r8 - 4)
    ).astype(BF16)
    push(0, 0, 2, up_a, dn_a, up_b, dn_b)

    def project(da, db):
        if db:
            wait(da, db, 0)
        t = at(da, db)
        acc[...] += dot(xfull[t, :L], w_v[pl.ds(pl.multiple_of(t * W, W), W), :])
        stat[...] += xfull[t, L:].astype(F32)

    for one in load_w:
        one.wait()
    project(0, 0)
    wait(-1, 0, 1)
    push(-1, 0, 1, up_a, up_b, dn_b)
    wait(1, 0, 1)
    push(1, 0, 1, up_b, dn_b)
    wait(0, -1, 1)
    push(0, -1, 1, up_b)
    wait(0, 1, 1)
    wait(1, 0, 2)
    push(1, 0, 2, dn_a, up_b, dn_b)
    wait(-1, 0, 2)
    push(-1, 0, 2, up_b, dn_b)
    wait(0, 1, 2)
    push(0, 1, 2, dn_b)
    wait(0, -1, 2)
    project(1, 0)
    project(-1, 0)
    for h in (1, 2):
        wait(2, 0, h)
        push(2, 0, h, up_b, dn_b)
    for da in (-1, 1):
        wait(da, -1, 1)
        push(da, -1, 1, up_b)
        wait(da, 1, 1)
    for da in (-1, 1):
        wait(da, 1, 2)
        push(da, 1, 2, dn_b)
        wait(da, -1, 2)
    wait(0, 2, 1)
    wait(0, 2, 2)
    for one in ((0, 1), (0, -1), (2, 0), (0, 2), (1, 1), (1, -1)):
        project(*one)
    wait(2, -1, 1)
    push(2, -1, 1, up_b)
    wait(2, 1, 1)
    wait(2, 1, 2)
    push(2, 1, 2, dn_b)
    wait(2, -1, 2)
    project(-1, 1)
    project(-1, -1)
    project(2, 1)
    project(2, -1)
    for da in (-1, 1):
        wait(da, 2, 1)
        wait(da, 2, 2)
        project(da, 2)
    for one in load_o:
        one.wait()
    for i in range(len(PEERS)):
        for db in range(4):
            w_wait(i, db)
    wait(2, 2, 1)
    wait(2, 2, 2)
    project(2, 2)

    sums = stat[...]

    def whole(r):
        return jnp.concatenate(
            [sums[r:r + 1, :] + sums[r + 2:r + 3, :],
             sums[r + 1:r + 2, :L - W] + sums[r + 3:r + 4, :L - W]], axis=1
        )

    rv = jnp.where(is_img_r, lax.rsqrt(whole(0) / D + EPS), 1.0)
    rd = lax.rsqrt(rv * rv * whole(4) / D + EPS)
    cols = jnp.transpose(jnp.where(iota((8, L), 0) == 0, rv * rd, rv))
    qkv = (acc[...] * cols[:, 0:1]).astype(BF16)
    queries = dot(to_pos[...], qkv[:, :HD]).astype(BF16)

    def c_copy(b, i):
        block = ctx.at[pl.ds(*Q_PARTS[b]), heads]
        return pltpu.make_async_remote_copy(
            src_ref=block, dst_ref=block, send_sem=c_send.at[b, i], recv_sem=c_recv.at[b, i],
            device_id={"tensor": at(PEERS[i], 0)}, device_id_type=MESH,
        )

    def c_wait(b, i):
        cols = pl.ds(pl.multiple_of(((pa - PEERS[i]) & 3) * HD, HD), HD)
        block = ctx.at[pl.ds(*Q_PARTS[b]), cols]
        pltpu.make_async_remote_copy(
            src_ref=block, dst_ref=block, send_sem=c_send.at[b, i], recv_sem=c_recv.at[b, i],
            device_id={"tensor": at(-PEERS[i], 0)}, device_id_type=MESH,
        ).wait_recv()

    def o_copy(b, i):
        rows = pl.ds(*Q_PARTS[b])
        return pltpu.make_async_remote_copy(
            src_ref=part.at[i, rows], dst_ref=part_in.at[i, rows], send_sem=o_send.at[b, i],
            recv_sem=o_recv.at[b, i], device_id={"tensor": at(0, PEERS[i])}, device_id_type=MESH,
        )

    both = [(b, i) for b in range(len(Q_PARTS)) for i in range(len(PEERS))]
    for b, (lo, n) in enumerate(Q_PARTS):
        scores = dot_nt(queries[lo:lo + n], qkv[:, HD:2 * HD]) * (HD ** -0.5)
        at_q = (iota((n, L), 0) + lo).astype(F32)
        scores = jnp.where((at_q >= pos_r) & (bad_r < 0.5), scores, -1e30)
        expo = jnp.exp(scores - jnp.max(scores, axis=-1, keepdims=True))
        probs = (expo / jnp.sum(expo, axis=-1, keepdims=True)).astype(BF16)
        ctx[lo:lo + n, heads] = dot(probs, qkv[:, 2 * HD:]).astype(BF16)
        for i in range(len(PEERS)):
            c_copy(b, i).start()
    oacc[...] = dot(to_pos[...], (xraw[...] * cols[:, 1:2]).astype(BF16))
    for b, (lo, n) in enumerate(Q_PARTS):
        for i in range(len(PEERS)):
            c_wait(b, i)
        for i, db in enumerate(PEERS):
            part[i, lo:lo + n] = dot(ctx[lo:lo + n], w_blk[(pb + db) & 3]).astype(BF16)
            o_copy(b, i).start()
    for b, (lo, n) in enumerate(Q_PARTS):
        oacc[lo:lo + n] += dot(ctx[lo:lo + n], w_blk[pb])
    for b, (lo, n) in enumerate(Q_PARTS):
        total = oacc[lo:lo + n]
        for i in range(len(PEERS)):
            o_copy(b, i).wait_recv()
            total = total + part_in[i, lo:lo + n].astype(F32)
        out_r[lo:lo + n] = total.astype(BF16)

    swap.wait_send()
    for e in range(1, NZ):
        packet(e).wait_send()
    for i in range(len(PEERS)):
        for db in range(4):
            w_copy(i, db).wait_send()
    for b, i in both:
        c_copy(b, i).wait_send()
        o_copy(b, i).wait_send()
    for one in sent:
        one.wait_send()


def body(text, patches, grids, image_request, slot_start, vis_gain, dec_gain, w_qkv, w_out):
    vmem = pl.BlockSpec(memory_space=pltpu.VMEM)
    hbm = pl.BlockSpec(memory_space=pl.ANY)
    dma = pltpu.SemaphoreType.DMA
    return pl.pallas_call(
        kernel,
        out_shape=jax.ShapeDtypeStruct((L, W), BF16),
        in_specs=[hbm, hbm, vmem, vmem, vmem, vmem, vmem, hbm, hbm],
        out_specs=vmem,
        scratch_shapes=[
            pltpu.VMEM((L, W), BF16),
            pltpu.VMEM((6, 6, IMG, W), BF16),
            pltpu.VMEM((D, 3 * HD), BF16),
            pltpu.VMEM((4, 4 * HD, W), BF16),
            pltpu.VMEM((CELLS, 2, IMG, W), BF16),
            pltpu.VMEM((NZ * PACK, HD), F32),
            pltpu.VMEM((NZ, PACK, HD), BF16),
            pltpu.VMEM((NZ, PACK, HD), BF16),
            pltpu.VMEM((L, L), BF16),
            pltpu.VMEM((L, L), BF16),
            pltpu.VMEM((L, W), F32),
            pltpu.VMEM((L, W), BF16),
            pltpu.VMEM((L, W), BF16),
            pltpu.VMEM((NT, L + 8, W), BF16),
            pltpu.VMEM((L, 4 * HD), BF16),
            pltpu.VMEM((3, L, W), BF16),
            pltpu.VMEM((3, L, W), BF16),
            pltpu.VMEM((L, 3 * HD), F32),
            pltpu.VMEM((L, W), F32),
            pltpu.VMEM((8, W), F32),
            dma((9,)), dma((2,)), dma((3, 4)), dma((3, 4)), dma((NZ,)), dma((NZ,)),
            dma((48,)), dma((NT, 3)), dma((2, 3)), dma((2, 3)), dma((2, 3)), dma((2, 3)),
        ],
        compiler_params=pltpu.CompilerParams(
            collective_id=0, has_side_effects=True, vmem_limit_bytes=62 * 2**20
        ),
    )(
        text,
        patches.transpose(1, 2, 0, 3),
        grids.T,
        image_request.reshape(1, -1),
        slot_start.reshape(1, -1),
        vis_gain.reshape(-1, HD),
        dec_gain.reshape(-1, HD),
        w_qkv.transpose(1, 0, 2),
        w_out,
    )


def solution(mesh):
    in_specs = (
        P("req", "tensor"),
        P("req", None, None, "tensor"),
        P(),
        P(),
        P(),
        P("tensor"),
        P(),
        P(None, None, "tensor"),
        P("tensor", None),
    )
    return jax.shard_map(
        body, mesh=mesh, in_specs=in_specs, out_specs=P("req", "tensor"), check_vma=False
    )
```

time: 84.4 us -> 63.9 us (0.76)
  the two profiles are of different devices: /device:TPU:8 before, /device:TPU:1 now
where the time goes in v4:
time: 63.9 us; the launch traced here: 63.3 us
  Pallas kernels  61.7 us (97%)
  local copies, waits for them, and re-layouts  1.62 us (3%)
    pallas_call x1, Pallas kernels, body(): pl.pallas_call(kernel, out_shape=jax.ShapeDtypeStruct((L, W), BF16), in_s...  61.7 us
    unnamed x1, local copies, waits for them, and re-layouts  1.62 us

profile of v4, /device:TPU:1, one launch (start us, length us, event | category | flops | bytes accessed | tf_op | source)
XLA Modules:
  0.0 63.3 jit_solution(6320816827401351486)
XLA Ops:
  0.0 61.7 %shard_map.91 = bf16[384,256]{1,0:T(8,128)(2,1)} custom-call(bf16[384,256]{1,0:T(8,128)(2,1)} %text_h.1, bf16[6,6,32,256]{3,2,1,0:T(8,128)(2,1)} %bitcast.8, s32[2,1024]{1,0:T(2,128)} %bitcast.9, s32[1,1024]{1,0:T(1,128)} %bitcast.11, s32[1,1024]{1,0:T(1,128)} %bitcast.12, bf16[2,128]{1,0:T(2,128)(2,1)} %bitcast.13, bf16[32,128]{1,0:T(8,128)(2,1)} %bitcast.10, ...), custom_call_target="tpu_custom_call" | custom-call | tf_op jit(solution)/shard_map/pallas_call | solution.py:466
  61.7 1.6 %copy.11 = bf16[384,256]{1,0:T(8,128)(2,1)} copy(bf16[384,256]{1,0:T(8,128)(2,1)} %shard_map.91) | data formatting | bytes 393216

commit v5 on v4

--- a/solution.py
+++ b/solution.py
@@ -121,14 +121,18 @@
 
     req = req_r[...]
     req8 = jnp.broadcast_to(req.astype(F32), (8, NR * IMG)).astype(BF16)
-    ours = (
-        iota((2 * IMG, NR * IMG), 1) == me_z * 2 * IMG + iota((2 * IMG, NR * IMG), 0)
-    ).astype(BF16)
-    goes = dot_nt(req8, ours)[0:1, :]
-    row_s = (iota((NR, 2 * IMG), 0) >= NZ).astype(jnp.int32)
-    col_s = (iota((NR, 2 * IMG), 1) >= IMG).astype(jnp.int32)
-    wanted = ((iota((NR, 2 * IMG), 0) - NZ * row_s) * 2 + core).astype(F32)
-    pick = ((row_s == col_s) & (wanted == goes)).astype(BF16)
+
+    def pack(s):
+        first = (me_z * 2 + s) * IMG
+        ours = (iota((IMG, NR * IMG), 1) == first + iota((IMG, NR * IMG), 0)).astype(BF16)
+        goes = dot_nt(req8, ours)[0:1, :]
+        return ((iota((NZ, IMG), 0) * 2 + core).astype(F32) == goes).astype(BF16)
+
+    def stage_rows(s, pick):
+        for c in range(CELLS):
+            rows = dot(pick, pool[c, s])
+            stage_f[pl.ds(s * CELLS + c, NZ, stride=PACK), :] = rows[:, :HD]
+            stage_f[pl.ds((2 + s) * CELLS + c, NZ, stride=PACK), :] = rows[:, HD:]
 
     load_p.wait()
     for c in range(CELLS):
@@ -140,32 +144,8 @@
         pool[c, core] = (total * 0.25).astype(BF16)
     stage_f[...] = jnp.zeros_like(stage_f)
 
-    pl.semaphore_wait(barrier, NZ - 1 + 1 + 2 * len(PEERS))
-
-    swap = pltpu.make_async_remote_copy(
-        src_ref=pool.at[:, core], dst_ref=pool.at[:, core], send_sem=p_sem.at[0],
-        recv_sem=p_sem.at[1], device_id={"req": sibling}, device_id_type=MESH,
-    )
-    swap.start()
-    swap.wait_recv()
-    for c in range(CELLS):
-        sent = dot(pick, pool[c].reshape(2 * IMG, W))
-        for s in range(2):
-            rows = sent[s * NZ:(s + 1) * NZ]
-            stage_f[pl.ds(s * CELLS + c, NZ, stride=PACK), :] = rows[:, :HD]
-            stage_f[pl.ds((2 + s) * CELLS + c, NZ, stride=PACK), :] = rows[:, HD:]
-    stage[...] = stage_f[...].astype(BF16).reshape(NZ, PACK, HD)
-
-    def packet(e):
-        to = (me_z + shift_of(e) + NZ) & (NZ - 1)
-        return pltpu.make_async_remote_copy(
-            src_ref=stage.at[to], dst_ref=recv.at[mirror(e)], send_sem=a_send.at[e],
-            recv_sem=a_recv.at[mirror(e)], device_id={"req": to * 2 + core}, device_id_type=MESH,
-        )
-
-    for e in range(NZ - 1, 0, -1):
-        packet(e).start()
-    recv[0] = stage[me_z]
+    stage_rows(core, pack(core))
+    other = pack(1 - core)
 
     row = iota((8, NR * IMG), 0)
     start = jnp.broadcast_to(slot_r[...], (8, NR * IMG))
@@ -243,6 +223,17 @@
             r == 0, hi[:, :W], jnp.where(r == 1, wide(hi), jnp.where(r == 2, lo[:, :W], wide(lo)))
         )
 
+    swap = pltpu.make_async_remote_copy(
+        src_ref=pool.at[:, core], dst_ref=pool.at[:, core], send_sem=p_sem.at[0],
+        recv_sem=p_sem.at[1], device_id={"req": sibling}, device_id_type=MESH,
+    )
+    def packet(e):
+        to = (me_z + shift_of(e) + NZ) & (NZ - 1)
+        return pltpu.make_async_remote_copy(
+            src_ref=stage.at[to], dst_ref=recv.at[mirror(e)], send_sem=a_send.at[e],
+            recv_sem=a_recv.at[mirror(e)], device_id={"req": to * 2 + core}, device_id_type=MESH,
+        )
+
     def put(x, rows):
         xfull[me_t, rows] = (x * gd).astype(BF16)
         sq_r[rows] = (x * x).astype(BF16)
@@ -295,14 +286,24 @@
 
     sq_i[:TEXT] = jnp.zeros((TEXT, W), BF16)
     put(xraw[:TEXT], slice(0, TEXT))
+    to_pos[...] = (iota((L, L), 0).astype(F32) == pos_r).astype(BF16)
+    stat[...] = jnp.zeros_like(stat)
+    acc[...] = jnp.zeros_like(acc)
     ring_b = tuple((0, d) for d in PEERS)
+
+    pl.semaphore_wait(barrier, NZ - 1 + 1 + 2 * len(PEERS))
+
+    swap.start()
     push(0, 0, 0, *((d, 0) for d in PEERS), *ring_b)
     for i in range(len(PEERS)):
         for db in range(4):
             w_copy(i, db).start()
-    to_pos[...] = (iota((L, L), 0).astype(F32) == pos_r).astype(BF16)
-    stat[...] = jnp.zeros_like(stat)
-    acc[...] = jnp.zeros_like(acc)
+    swap.wait_recv()
+    stage_rows(1 - core, other)
+    stage[...] = stage_f[...].astype(BF16).reshape(NZ, PACK, HD)
+    for e in range(NZ - 1, 0, -1):
+        packet(e).start()
+    recv[0] = stage[me_z]
     for da in PEERS[::-1]:
         wait(da, 0, 0)
         push(da, 0, 0, *ring_b)

time: 63.9 us -> 61.2 us (0.958)
  Pallas kernels: 61.7 us -> 58.8 us
    pallas_call x1, Pallas kernels: 61.7 us -> 58.8 us  [body(): pl.pallas_call(kernel, out_shape=jax.ShapeDtypeStruct((L, W), BF16), in_s...]
where the time goes in v5:
time: 61.2 us; the launch traced here: 60.4 us
  Pallas kernels  58.8 us (96%)
  local copies, waits for them, and re-layouts  1.62 us (3%)
    pallas_call x1, Pallas kernels, body(): pl.pallas_call(kernel, out_shape=jax.ShapeDtypeStruct((L, W), BF16), in_s...  58.8 us
    unnamed x1, local copies, waits for them, and re-layouts  1.62 us

profile of v5, /device:TPU:1, one launch (start us, length us, event | category | flops | bytes accessed | tf_op | source)
XLA Modules:
  0.0 60.4 jit_solution(10036345959950695374)
XLA Ops:
  0.0 58.8 %shard_map.91 = bf16[384,256]{1,0:T(8,128)(2,1)} custom-call(bf16[384,256]{1,0:T(8,128)(2,1)} %text_h.1, bf16[6,6,32,256]{3,2,1,0:T(8,128)(2,1)} %bitcast.8, s32[2,1024]{1,0:T(2,128)} %bitcast.9, s32[1,1024]{1,0:T(1,128)} %bitcast.11, s32[1,1024]{1,0:T(1,128)} %bitcast.12, bf16[2,128]{1,0:T(2,128)(2,1)} %bitcast.13, bf16[32,128]{1,0:T(8,128)(2,1)} %bitcast.10, ...), custom_call_target="tpu_custom_call" | custom-call | tf_op jit(solution)/shard_map/pallas_call | solution.py:467
  58.8 1.6 %copy.11 = bf16[384,256]{1,0:T(8,128)(2,1)} copy(bf16[384,256]{1,0:T(8,128)(2,1)} %shard_map.91) | data formatting | bytes 393216

commit v6 on v5

--- a/solution.py
+++ b/solution.py
@@ -300,7 +300,7 @@
             w_copy(i, db).start()
     swap.wait_recv()
     stage_rows(1 - core, other)
-    stage[...] = stage_f[...].astype(BF16).reshape(NZ, PACK, HD)
+    stage[...] = stage_f[:NZ * PACK].astype(BF16).reshape(NZ, PACK, HD)
     for e in range(NZ - 1, 0, -1):
         packet(e).start()
     recv[0] = stage[me_z]
@@ -475,7 +475,7 @@
             pltpu.VMEM((D, 3 * HD), BF16),
             pltpu.VMEM((4, 4 * HD, W), BF16),
             pltpu.VMEM((CELLS, 2, IMG, W), BF16),
-            pltpu.VMEM((NZ * PACK, HD), F32),
+            pltpu.VMEM(((NZ + 1) * PACK, HD), F32),
             pltpu.VMEM((NZ, PACK, HD), BF16),
             pltpu.VMEM((NZ, PACK, HD), BF16),
             pltpu.VMEM((L, L), BF16),

time: 61.2 us -> 61.2 us (level)
  no operation moved by 1% of the time
where the time goes in v6:
time: 61.2 us; the launch traced here: 60.4 us
  Pallas kernels  58.8 us (96%)
  local copies, waits for them, and re-layouts  1.62 us (3%)
    pallas_call x1, Pallas kernels, body(): pl.pallas_call(kernel, out_shape=jax.ShapeDtypeStruct((L, W), BF16), in_s...  58.8 us
    unnamed x1, local copies, waits for them, and re-layouts  1.62 us

profile of v6, /device:TPU:1, one launch (start us, length us, event | category | flops | bytes accessed | tf_op | source)
XLA Modules:
  0.0 60.4 jit_solution(1226175803415389340)
XLA Ops:
  0.0 58.8 %shard_map.91 = bf16[384,256]{1,0:T(8,128)(2,1)} custom-call(bf16[384,256]{1,0:T(8,128)(2,1)} %text_h.1, bf16[6,6,32,256]{3,2,1,0:T(8,128)(2,1)} %bitcast.8, s32[2,1024]{1,0:T(2,128)} %bitcast.9, s32[1,1024]{1,0:T(1,128)} %bitcast.11, s32[1,1024]{1,0:T(1,128)} %bitcast.12, bf16[2,128]{1,0:T(2,128)(2,1)} %bitcast.13, bf16[32,128]{1,0:T(8,128)(2,1)} %bitcast.10, ...), custom_call_target="tpu_custom_call" | custom-call | tf_op jit(solution)/shard_map/pallas_call | solution.py:467
  58.8 1.6 %copy.11 = bf16[384,256]{1,0:T(8,128)(2,1)} copy(bf16[384,256]{1,0:T(8,128)(2,1)} %shard_map.91) | data formatting | bytes 393216

commit v7 on v6

--- a/solution.py
+++ b/solution.py
@@ -23,7 +23,7 @@
 BF16 = jnp.bfloat16
 EARLY, SPLIT = TEXT, TEXT + 2 * GROUP
 X_PARTS = ((0, EARLY), (EARLY, SPLIT - EARLY), (SPLIT, L + 8 - SPLIT))
-Q_PARTS = ((0, L // 2), (L // 2, L // 2))
+Q_PARTS = ((0, 128), (128, 128), (256, 128))
 PEERS = (2, 1, -1)
 
 
@@ -345,8 +345,6 @@
     wait(0, 1, 2)
     push(0, 1, 2, dn_b)
     wait(0, -1, 2)
-    project(1, 0)
-    project(-1, 0)
     for h in (1, 2):
         wait(2, 0, h)
         push(2, 0, h, up_b, dn_b)
@@ -358,9 +356,7 @@
         wait(da, 1, 2)
         push(da, 1, 2, dn_b)
         wait(da, -1, 2)
-    wait(0, 2, 1)
-    wait(0, 2, 2)
-    for one in ((0, 1), (0, -1), (2, 0), (0, 2), (1, 1), (1, -1)):
+    for one in ((1, 0), (-1, 0), (0, 1), (0, -1)):
         project(*one)
     wait(2, -1, 1)
     push(2, -1, 1, up_b)
@@ -368,10 +364,10 @@
     wait(2, 1, 2)
     push(2, 1, 2, dn_b)
     wait(2, -1, 2)
-    project(-1, 1)
-    project(-1, -1)
-    project(2, 1)
-    project(2, -1)
+    wait(0, 2, 1)
+    wait(0, 2, 2)
+    for one in ((2, 0), (0, 2), (1, 1), (1, -1), (-1, 1), (-1, -1), (2, 1), (2, -1)):
+        project(*one)
     for da in (-1, 1):
         wait(da, 2, 1)
         wait(da, 2, 2)
@@ -491,7 +487,7 @@
             pltpu.VMEM((L, W), F32),
             pltpu.VMEM((8, W), F32),
             dma((9,)), dma((2,)), dma((3, 4)), dma((3, 4)), dma((NZ,)), dma((NZ,)),
-            dma((48,)), dma((NT, 3)), dma((2, 3)), dma((2, 3)), dma((2, 3)), dma((2, 3)),
+            dma((48,)), dma((NT, 3)), dma((3, 3)), dma((3, 3)), dma((3, 3)), dma((3, 3)),
         ],
         compiler_params=pltpu.CompilerParams(
             collective_id=0, has_side_effects=True, vmem_limit_bytes=62 * 2**20

time: 61.2 us -> 61 us (level)
  no operation moved by 1% of the time
where the time goes in v7:
time: 61 us; the launch traced here: 60.2 us
  Pallas kernels  58.5 us (96%)
  local copies, waits for them, and re-layouts  1.62 us (3%)
    pallas_call x1, Pallas kernels, body(): pl.pallas_call(kernel, out_shape=jax.ShapeDtypeStruct((L, W), BF16), in_s...  58.5 us
    unnamed x1, local copies, waits for them, and re-layouts  1.62 us

profile of v7, /device:TPU:1, one launch (start us, length us, event | category | flops | bytes accessed | tf_op | source)
XLA Modules:
  0.0 60.2 jit_solution(13640611822742477367)
XLA Ops:
  0.0 58.5 %shard_map.91 = bf16[384,256]{1,0:T(8,128)(2,1)} custom-call(bf16[384,256]{1,0:T(8,128)(2,1)} %text_h.1, bf16[6,6,32,256]{3,2,1,0:T(8,128)(2,1)} %bitcast.8, s32[2,1024]{1,0:T(2,128)} %bitcast.9, s32[1,1024]{1,0:T(1,128)} %bitcast.11, s32[1,1024]{1,0:T(1,128)} %bitcast.12, bf16[2,128]{1,0:T(2,128)(2,1)} %bitcast.13, bf16[32,128]{1,0:T(8,128)(2,1)} %bitcast.10, ...), custom_call_target="tpu_custom_call" | custom-call | tf_op jit(solution)/shard_map/pallas_call | solution.py:463
  58.6 1.6 %copy.11 = bf16[384,256]{1,0:T(8,128)(2,1)} copy(bf16[384,256]{1,0:T(8,128)(2,1)} %shard_map.91) | data formatting | bytes 393216
